TPU v7x, 512 devices: a whole 4x8x8 slice. The times are simulated.
512 devices in a mesh: vertex: 64 (over z, y), view: 8 (over x, core).
Axes of the slice: x: 4, y: 8, z: 8, core: 2. Of those that a mesh axis runs over, the one named last changes fastest.
Arguments:
- coeffs: bfloat16 [512], P('view'), may hold values from -4 to 4
- shape_basis: bfloat16 [512, 3, 65536], P('view', None, 'vertex'), may hold values from -0.25 to 0.25
- rest_pose: float32 [3, 65536], P(None, 'vertex'), may hold values from -5 to 5
- triangles: int32 [3, 131072], P(None, 'vertex'), may hold values from 0 to 1023
- fetch_list: int32 [512, 64, 4], P(('vertex', 'view')), may hold values from -1 to 15, as said below
- tile_cover: int32 [16384, 8], P(('vertex', 'view')), may hold values from 0 to 255, as said below
- pix_slot: int32 [16384, 256], P(('vertex', 'view')), may hold values from 0 to 1023
- barycentric: float32 [16384, 3, 256], P(('vertex', 'view')), as said below
- camera: float32 [16384, 12], P(('vertex', 'view')), may hold values from -2 to 2
- target: float32 [16384, 3, 256], P(('vertex', 'view')), may hold values from -1 to 1
Outputs:
- photo_loss: float32 [], replicated
- vertex_grad: float32 [3, 65536], P(None, 'vertex')
- coeff_grad: float32 [512], P('view')
Inputs may be any that keep to these rules, and one draw needn't show every extreme that they name: Triangle t lies in vertex shard t // 2048; its corners are the vertices triangles[c, t] + (t // 2048) * 1024 of that shard. Let u = o // 8 for owner o. Each row fetch_list[o, h] names distinct blocks of shard h, filled from the front and -1 after. A row is empty unless (h - u) mod 64 is one of j - 3 for j = 0 .. 8 - 2 (taken mod 64) or 32; other rows may be empty too, and every owner has some shard with all 4 entries filled. `tile_cover`: entry e of a tile names entry e % 4 of row e // 4 of the fetch list of the tile's owner (tile t belongs to owner t // 32); that entry is always filled. `pix_slot`: slot q names triangle q % 128 of the block given by the tile's coverage entry q // 128. `barycentric`: the three weights of a pixel are positive and sum to one.
All inputs are finite; a program needn't handle non-finite values.
Results may differ from a plain program's by a relative error of at most 0.0003.
Values sent between devices are 32-bit elements; how exact they have to be, the bound alone decides.
No kernel may reach another device: no remote copies, remote signals or barrier semaphores. Data moves between devices by JAX's collectives and lax.ppermute only.
A program may use at most 64 MiB of HBM per device.

v0:
```python
import math

import jax
import jax.numpy as jnp
from jax import lax
from jax.sharding import PartitionSpec as P

BLOCK = 128


SMOOTH = 0.1


def copy_for_each(array, axis):
    size = lax.axis_size(axis)
    return lax.all_to_all(
        jnp.broadcast_to(array[None], (size, *array.shape)), axis, 0, 0, tiled=True
    )


def of_everyone(array, axis):
    return copy_for_each(array, axis).sum(axis=0)


def packed_total(arrays, axis):
    flat, at, done = (jnp.concatenate([a.reshape(-1) for a in arrays]), 0, [])
    running = of_everyone(flat, axis)
    for a in arrays:
        done.append(running[at : at + a.size].reshape(a.shape))
        at += a.size
    return tuple(done)


def split_parts(values):
    high = values.astype(jnp.bfloat16)
    rest = values - lax.optimization_barrier(high).astype(jnp.float32)
    middle = rest.astype(jnp.bfloat16)
    lowest = (rest - lax.optimization_barrier(middle).astype(jnp.float32)).astype(jnp.bfloat16)
    return jnp.concatenate([high, middle, lowest], axis=0)


def join_parts(summed):
    rows = summed.shape[0] // 3
    return summed[0:rows] + summed[rows : 2 * rows] + summed[2 * rows : 3 * rows]


def corner_blocks_of(triangles, vert_count):
    tri_count = triangles.shape[1]
    width = math.gcd(tri_count, 512)
    pieces = jnp.transpose(triangles.reshape(3, tri_count // width, width), (1, 0, 2))
    vertex_ids = jnp.arange(vert_count, dtype=jnp.int32)[:, None]
    return (pieces, vertex_ids, width)


def gather_corners(positions, triangles):
    vert_count = positions.shape[1]
    tri_count = triangles.shape[1]
    pieces, vertex_ids, width = corner_blocks_of(triangles, vert_count)
    parts = split_parts(positions)

    def gather_one_piece(piece):
        picked = []
        for corner_id in range(3):
            onehot = (vertex_ids == piece[corner_id][None, :]).astype(jnp.bfloat16)
            summed = jnp.dot(parts, onehot, preferred_element_type=jnp.float32)
            picked.append(join_parts(summed))
        return jnp.stack(picked, axis=0)

    gathered = lax.map(gather_one_piece, pieces)
    return jnp.transpose(gathered, (1, 2, 0, 3)).reshape(3, 3, tri_count)


def spread_corners(corner_grad, triangles, vert_count):
    tri_count = triangles.shape[1]
    pieces, vertex_ids, width = corner_blocks_of(triangles, vert_count)
    grad_pieces = jnp.transpose(corner_grad.reshape(3, 3, tri_count // width, width), (2, 0, 1, 3))

    def spread_one_piece(total, items):
        piece, grads = items
        for corner_id in range(3):
            onehot = (vertex_ids == piece[corner_id][None, :]).astype(jnp.bfloat16)
            parts = split_parts(grads[corner_id])
            summed = lax.dot_general(
                parts, onehot, (((1,), (1,)), ((), ())), preferred_element_type=jnp.float32
            )
            total = total + join_parts(summed)
        return (total, None)

    start = jnp.zeros((3, vert_count), jnp.float32)
    total, unused = lax.scan(spread_one_piece, start, (pieces, grad_pieces))
    return total


def shade_group(items):
    rows, slots, weights, lens, wanted = items
    group = rows.shape[0]
    slot_count = rows.shape[2]
    onehot = (slots[:, None, :] == jnp.arange(slot_count, dtype=jnp.int32)[None, :, None]).astype(
        jnp.float32
    )
    corners = jnp.einsum("gdq,gqp->gdp", rows, onehot, precision=lax.Precision.HIGHEST)
    surface = weights[:, 0:1, :] * corners[:, 0:3]
    surface = surface + weights[:, 1:2, :] * corners[:, 3:6]
    surface = surface + weights[:, 2:3, :] * corners[:, 6:9]
    matrix = lens[:, :9].reshape(group, 3, 3)
    shifted = lens[:, 9:12]
    linear = matrix[:, :, 0, None] * surface[:, 0][:, None, :]
    linear = linear + matrix[:, :, 1, None] * surface[:, 1][:, None, :]
    linear = linear + matrix[:, :, 2, None] * surface[:, 2][:, None, :]
    linear = linear + shifted[:, :, None]
    shaded = jnp.tanh(linear)
    differ = shaded - wanted
    spread = jnp.sqrt(differ * differ + SMOOTH * SMOOTH)
    grad_linear = differ / spread * (1.0 - shaded * shaded)
    grad_surface = jnp.stack(
        [jnp.sum(matrix[:, :, dim_id, None] * grad_linear, axis=1) for dim_id in range(3)], axis=1
    )
    grad_corner = jnp.concatenate(
        [weights[:, corner_id : corner_id + 1, :] * grad_surface for corner_id in range(3)], axis=1
    )
    rows_grad = jnp.einsum("gdp,gqp->gdq", grad_corner, onehot, precision=lax.Precision.HIGHEST)
    return (jnp.sum(spread), rows_grad)


def shade_tiles(block_table, tile_cover, pix_slot, barycentric, camera, target):
    tile_count, cover_count = tile_cover.shape
    entry_count = block_table.shape[1]
    pick = (
        tile_cover[:, :, None] == jnp.arange(entry_count, dtype=jnp.int32)[None, None, :]
    ).astype(jnp.float32)
    rows = jnp.einsum("tne,del->tdnl", pick, block_table, precision=lax.Precision.HIGHEST)
    rows = rows.reshape(tile_count, 9, cover_count * BLOCK)
    group = math.gcd(tile_count, 4)
    turns = tile_count // group

    def split_tiles(values):
        return values.reshape((turns, group) + values.shape[1:])

    energies, rows_grads = lax.map(
        shade_group,
        (
            split_tiles(rows),
            split_tiles(pix_slot),
            split_tiles(barycentric),
            split_tiles(camera),
            split_tiles(target),
        ),
    )
    rows_grad = rows_grads.reshape(tile_count, 9, cover_count, BLOCK)
    grad_table = jnp.einsum("tne,tdnl->del", pick, rows_grad, precision=lax.Precision.HIGHEST)
    return (jnp.sum(energies), grad_table)


def per_device(
    coeffs,
    shape_basis,
    rest_pose,
    triangles,
    fetch_list,
    tile_cover,
    pix_slot,
    barycentric,
    camera,
    target,
):
    shape_rows = shape_basis.shape[0]
    vert_count = shape_basis.shape[2]
    flat_basis = shape_basis.reshape(shape_rows, 3 * vert_count)
    partial_value = jnp.dot(
        coeffs[None, :], flat_basis, preferred_element_type=jnp.float32
    ).reshape(3, vert_count)
    positions = rest_pose + of_everyone(partial_value, "view")
    tri_count = triangles.shape[1]
    block_count = tri_count // BLOCK
    corner_data = gather_corners(positions, triangles).reshape(9, block_count, BLOCK)
    holder_count = fetch_list.shape[1]
    slot_count = fetch_list.shape[2]
    onehot = (
        lax.all_to_all(fetch_list, "vertex", split_axis=1, concat_axis=1, tiled=True)[0][..., None]
        == jnp.arange(block_count, dtype=jnp.int32)
    ).astype(jnp.float32)
    fetched = lax.all_to_all(
        jnp.einsum("...b,dbl->d...l", onehot, corner_data, precision=lax.Precision.HIGHEST),
        "vertex",
        split_axis=1,
        concat_axis=1,
        tiled=True,
    )
    block_table = fetched.reshape(9, holder_count * slot_count, BLOCK)
    local_energy, grad_table = shade_tiles(
        block_table, tile_cover, pix_slot, barycentric, camera, target
    )
    grad_back = grad_table.reshape(9, holder_count, slot_count, BLOCK)
    returned, request_rows = (
        lax.all_to_all(grad_back, "vertex", split_axis=1, concat_axis=1, tiled=True),
        lax.all_to_all(fetch_list, "vertex", split_axis=1, concat_axis=1, tiled=True),
    )
    wanted_ids = request_rows[0].reshape(-1)
    onehot = (wanted_ids[None, :] == jnp.arange(block_count, dtype=jnp.int32)[:, None]).astype(
        jnp.float32
    )
    block_grad = jnp.einsum(
        "bn,dnl->dbl", onehot, returned.reshape(9, -1, BLOCK), precision=lax.Precision.HIGHEST
    )
    corner_grad = block_grad.reshape(3, 3, tri_count)
    vertex_part = spread_corners(corner_grad, triangles, vert_count)
    pixel_total = (
        tile_cover.shape[0] * pix_slot.shape[1] * lax.axis_size("vertex") * lax.axis_size("view")
    )
    vertex_grad, view_energy = (of_everyone(vertex_part, "view"), of_everyone(local_energy, "view"))
    coeff_grad, energy = packed_total(
        (
            jnp.dot(
                flat_basis.astype(jnp.float32),
                vertex_grad.reshape(-1),
                precision=lax.Precision.HIGHEST,
            ),
            view_energy,
        ),
        "vertex",
    )
    return (energy / pixel_total, vertex_grad, coeff_grad)


def solution(mesh):
    placed = (
        P("view"),
        P("view", None, "vertex"),
        P(None, "vertex"),
        P(None, "vertex"),
        P(("vertex", "view"), None, None),
        P(("vertex", "view"), None),
        P(("vertex", "view"), None),
        P(("vertex", "view"), None, None),
        P(("vertex", "view"), None),
        P(("vertex", "view"), None, None),
    )
    return jax.shard_map(
        per_device,
        mesh=mesh,
        in_specs=placed,
        out_specs=(P(), P(None, "vertex"), P("view")),
        check_vma=False,
    )
```

profile of v0, /device:TPU:1, one launch (start us, length us, event | category | flops | bytes accessed | tf_op | source)
XLA Modules:
  0.0 240.5 jit_solution(6502650781956241955)
XLA Ops:
  2.1 17.1 %all-to-all-start.1 = ((s32[1,64,4]{2,0,1:T(1,128)}), s32[1,64,4]{2,0,1:T(1,128)S(1)}, u32[]{:S(2)}, u32[]{:S(2)}) async-start(s32[1,64,4]{2,0,1:T(1,128)} %copy.71), calls=%async_computation.1 | async-start | bytes 65536 | tf_op jit(solution)/shard_map/all_to_all | solution.py:179
  20.0 10.0 %all-to-all-done.1 = s32[1,64,4]{2,0,1:T(1,128)S(1)} async-done(((s32[1,64,4]{2,0,1:T(1,128)}), s32[1,64,4]{2,0,1:T(1,128)S(1)}, u32[]{:S(2)}, u32[]{:S(2)}) %all-to-all-start.1) | async-done | bytes 1056 | tf_op jit(solution)/shard_map/all_to_all | solution.py:179
  30.7 6.4 %all-to-all-start = ((f32[8,3,1024]{2,1,0:T(4,128)}), f32[8,3,1024]{2,1,0:T(4,128)S(1)}, u32[]{:S(2)}, u32[]{:S(2)}) async-start(f32[8,3,1024]{2,1,0:T(4,128)} %broadcast_in_dim.32), calls=%async_computation | async-start | bytes 262144 | tf_op jit(solution)/shard_map/all_to_all | solution.py:16
  37.2 5.2 %all-to-all-done = f32[8,3,1024]{2,1,0:T(4,128)S(1)} async-done(((f32[8,3,1024]{2,1,0:T(4,128)}), f32[8,3,1024]{2,1,0:T(4,128)S(1)}, u32[]{:S(2)}, u32[]{:S(2)}) %all-to-all-start) | async-done | bytes 98336 | tf_op jit(solution)/shard_map/all_to_all | solution.py:16
  43.2 8.9 %while.37 = (s32[]{:T(128)}, f32[4,3,3,512]{3,2,1,0:T(4,128)S(1)}, s32[4,3,512]{2,1,0:T(4,128)}, bf16[9,1024]{1,0:T(8,128)(2,1)S(1)}, s32[]{:T(128)}, /*index=5*/s32[]{:T(128)}, s32[]{}, s32[]{}) while((s32[]{:T(128)}, f32[4,3,3,512]{3,2,1,0:T(4,128)S(1)}, s32[4,3,512]{2,1,0:T(4,128)}, bf16[9,1024]{1,0:T(8,128)(2,1)S(1)}, ...), condition=%wide.region_2.3_spmd.clone.clone, body=%wide.region_1.2_spmd.clone.clone.sunk | while | flops 29902852 | bytes 252037 | solution.py:69
  52.9 1.8 copy.73
  54.7 4.7 %all-to-all-start.2 = ((f32[9,64,4,128]{3,2,0,1:T(4,128)}), f32[9,64,4,128]{3,2,0,1:T(4,128)S(1)}, u32[]{:S(2)}, u32[]{:S(2)}) async-start(f32[9,64,4,128]{3,2,0,1:T(4,128)} %copy.73), calls=%async_computation.2 | async-start | bytes 2359296 | tf_op jit(solution)/shard_map/all_to_all | solution.py:182
  59.8 30.2 %all-to-all-done.2 = f32[9,64,4,128]{3,2,0,1:T(4,128)S(1)} async-done(((f32[9,64,4,128]{3,2,0,1:T(4,128)}), f32[9,64,4,128]{3,2,0,1:T(4,128)S(1)}, u32[]{:S(2)}, u32[]{:S(2)}) %all-to-all-start.2) | async-done | bytes 1179680 | tf_op jit(solution)/shard_map/all_to_all | solution.py:182
  93.3 55.8 %while.36 = (s32[]{:T(128)}, f32[8]{0:T(128)S(1)}, f32[8,4,9,1024]{3,2,1,0:T(8,128)}, f32[8,4,12]{2,1,0:T(4,128)S(1)}, f32[8,4,3,256]{3,1,0,2:T(4,128)S(1)}, /*i...) while((s32[]{:T(128)}, f32[8]{0:T(128)S(1)}, ...), condition=%wide.region_8.9_spmd, body=%wide.region_3.8_spmd.sunk | while | flops 228697088 | bytes 898413 | solution.py:139
  93.7 2.4 fusion.122
  97.6 2.7 %fusion.125 = f32[8,4,9,1024]{3,2,1,0:T(8,128)} fusion(f32[8,4,9,1024]{3,2,1,0:T(8,128)} %get-tuple-element.478, s32[]{:T(128)S(6)} %copy.144, s32[4,256]{1,0:T(4,128)S(1)} %dynamic-slice_bitcast_fusion.10, f32[4,3,256]{2,1,0:T(4,128)S(1)} %get-tuple-element.415, f32[4,3,256]{2,1,0:T(4,128)S(1)} %get-tuple-element.416, ...), kind=kOutput, calls=%fused_computation.88.clone.1 | convolution fusion | flops 114313216 | bytes 303108 | tf_op jit(solution)/shard_map/while/body/eval_jaxpr/gdp,gqp->gdq/dot_general | solution.py:121
  100.7 2.4 fusion.122
  104.6 2.7 %fusion.125 = f32[8,4,9,1024]{3,2,1,0:T(8,128)} fusion(f32[8,4,9,1024]{3,2,1,0:T(8,128)} %get-tuple-element.478, s32[]{:T(128)S(6)} %copy.144, s32[4,256]{1,0:T(4,128)S(1)} %dynamic-slice_bitcast_fusion.10, f32[4,3,256]{2,1,0:T(4,128)S(1)} %get-tuple-element.415, f32[4,3,256]{2,1,0:T(4,128)S(1)} %get-tuple-element.416, ...), kind=kOutput, calls=%fused_computation.88.clone.1 | convolution fusion | flops 114313216 | bytes 303108 | tf_op jit(solution)/shard_map/while/body/eval_jaxpr/gdp,gqp->gdq/dot_general | solution.py:121
  107.6 2.4 fusion.122
  111.6 2.7 %fusion.125 = f32[8,4,9,1024]{3,2,1,0:T(8,128)} fusion(f32[8,4,9,1024]{3,2,1,0:T(8,128)} %get-tuple-element.478, s32[]{:T(128)S(6)} %copy.144, s32[4,256]{1,0:T(4,128)S(1)} %dynamic-slice_bitcast_fusion.10, f32[4,3,256]{2,1,0:T(4,128)S(1)} %get-tuple-element.415, f32[4,3,256]{2,1,0:T(4,128)S(1)} %get-tuple-element.416, ...), kind=kOutput, calls=%fused_computation.88.clone.1 | convolution fusion | flops 114313216 | bytes 303108 | tf_op jit(solution)/shard_map/while/body/eval_jaxpr/gdp,gqp->gdq/dot_general | solution.py:121
  114.6 2.4 fusion.122
  118.5 2.7 %fusion.125 = f32[8,4,9,1024]{3,2,1,0:T(8,128)} fusion(f32[8,4,9,1024]{3,2,1,0:T(8,128)} %get-tuple-element.478, s32[]{:T(128)S(6)} %copy.144, s32[4,256]{1,0:T(4,128)S(1)} %dynamic-slice_bitcast_fusion.10, f32[4,3,256]{2,1,0:T(4,128)S(1)} %get-tuple-element.415, f32[4,3,256]{2,1,0:T(4,128)S(1)} %get-tuple-element.416, ...), kind=kOutput, calls=%fused_computation.88.clone.1 | convolution fusion | flops 114313216 | bytes 303108 | tf_op jit(solution)/shard_map/while/body/eval_jaxpr/gdp,gqp->gdq/dot_general | solution.py:121
  121.6 2.4 fusion.122
  125.5 2.7 %fusion.125 = f32[8,4,9,1024]{3,2,1,0:T(8,128)} fusion(f32[8,4,9,1024]{3,2,1,0:T(8,128)} %get-tuple-element.478, s32[]{:T(128)S(6)} %copy.144, s32[4,256]{1,0:T(4,128)S(1)} %dynamic-slice_bitcast_fusion.10, f32[4,3,256]{2,1,0:T(4,128)S(1)} %get-tuple-element.415, f32[4,3,256]{2,1,0:T(4,128)S(1)} %get-tuple-element.416, ...), kind=kOutput, calls=%fused_computation.88.clone.1 | convolution fusion | flops 114313216 | bytes 303108 | tf_op jit(solution)/shard_map/while/body/eval_jaxpr/gdp,gqp->gdq/dot_general | solution.py:121
  128.6 2.4 fusion.122
  132.5 2.7 %fusion.125 = f32[8,4,9,1024]{3,2,1,0:T(8,128)} fusion(f32[8,4,9,1024]{3,2,1,0:T(8,128)} %get-tuple-element.478, s32[]{:T(128)S(6)} %copy.144, s32[4,256]{1,0:T(4,128)S(1)} %dynamic-slice_bitcast_fusion.10, f32[4,3,256]{2,1,0:T(4,128)S(1)} %get-tuple-element.415, f32[4,3,256]{2,1,0:T(4,128)S(1)} %get-tuple-element.416, ...), kind=kOutput, calls=%fused_computation.88.clone.1 | convolution fusion | flops 114313216 | bytes 303108 | tf_op jit(solution)/shard_map/while/body/eval_jaxpr/gdp,gqp->gdq/dot_general | solution.py:121
  135.6 2.4 fusion.122
  139.5 2.7 %fusion.125 = f32[8,4,9,1024]{3,2,1,0:T(8,128)} fusion(f32[8,4,9,1024]{3,2,1,0:T(8,128)} %get-tuple-element.478, s32[]{:T(128)S(6)} %copy.144, s32[4,256]{1,0:T(4,128)S(1)} %dynamic-slice_bitcast_fusion.10, f32[4,3,256]{2,1,0:T(4,128)S(1)} %get-tuple-element.415, f32[4,3,256]{2,1,0:T(4,128)S(1)} %get-tuple-element.416, ...), kind=kOutput, calls=%fused_computation.88.clone.1 | convolution fusion | flops 114313216 | bytes 303108 | tf_op jit(solution)/shard_map/while/body/eval_jaxpr/gdp,gqp->gdq/dot_general | solution.py:121
  142.5 2.4 fusion.122
  146.5 2.7 %fusion.125 = f32[8,4,9,1024]{3,2,1,0:T(8,128)} fusion(f32[8,4,9,1024]{3,2,1,0:T(8,128)} %get-tuple-element.478, s32[]{:T(128)S(6)} %copy.144, s32[4,256]{1,0:T(4,128)S(1)} %dynamic-slice_bitcast_fusion.10, f32[4,3,256]{2,1,0:T(4,128)S(1)} %get-tuple-element.415, f32[4,3,256]{2,1,0:T(4,128)S(1)} %get-tuple-element.416, ...), kind=kOutput, calls=%fused_computation.88.clone.1 | convolution fusion | flops 114313216 | bytes 303108 | tf_op jit(solution)/shard_map/while/body/eval_jaxpr/gdp,gqp->gdq/dot_general | solution.py:121
  153.5 7.6 %all-to-all-start.3 = ((f32[9,64,4,128]{3,2,0,1:T(4,128)}), f32[9,64,4,128]{3,2,0,1:T(4,128)S(1)}, u32[]{:S(2)}, u32[]{:S(2)}) async-start(f32[9,64,4,128]{3,2,0,1:T(4,128)} %copy.83), calls=%async_computation.3 | async-start | bytes 2359296 | tf_op jit(solution)/shard_map/all_to_all | solution.py:195
  163.1 26.7 %all-to-all-done.3 = f32[9,64,4,128]{3,2,0,1:T(4,128)S(1)} async-done(((f32[9,64,4,128]{3,2,0,1:T(4,128)}), f32[9,64,4,128]{3,2,0,1:T(4,128)S(1)}, u32[]{:S(2)}, u32[]{:S(2)}) %all-to-all-start.3) | async-done | bytes 1179680 | tf_op jit(solution)/shard_map/all_to_all | solution.py:195
  191.0 8.2 %all-to-all-start.5 = ((f32[8,1,1]{2,1,0:T(1,128)}), f32[8,1,1]{2,1,0:T(1,128)S(1)}, u32[]{:S(2)}, u32[]{:S(2)}) async-start(f32[8,1,1]{2,1,0:T(1,128)} %broadcast_in_dim.34), calls=%async_computation.5 | async-start | bytes 8192 | tf_op jit(solution)/shard_map/all_to_all | solution.py:16
  200.1 9.4 %while.38 = (s32[]{:T(128)}, f32[3,1024]{1,0:T(4,128)S(1)}, f32[4,3,3,512]{3,2,1,0:T(4,128)S(1)}, s32[4,3,512]{2,1,0:T(4,128)}, s32[]{:T(128)}, /*index=5*/s32[]{:T(128)}, s32[]{}, s32[]{}) while((s32[]{:T(128)}, f32[3,1024]{1,0:T(4,128)S(1)}, f32[4,3,3,512]{3,2,1,0:T(4,128)S(1)}, s32[4,3,512]{2,1,0:T(4,128)}, ...), condition=%wide.region_10.11_spmd.clone.clone, body=%wide.region_9.10_spmd.clone.clone.sunk | while | flops 30034948 | bytes 393391 | solution.py:90
  210.2 4.8 %all-to-all-start.4 = ((f32[8,3,1024]{2,1,0:T(4,128)}), f32[8,3,1024]{2,1,0:T(4,128)S(1)}, u32[]{:S(2)}, u32[]{:S(2)}) async-start(f32[8,3,1024]{2,1,0:T(4,128)} %broadcast_in_dim.33), calls=%async_computation.4 | async-start | bytes 262144 | tf_op jit(solution)/shard_map/all_to_all | solution.py:16
  215.6 4.6 %all-to-all-done.4 = f32[8,3,1024]{2,1,0:T(4,128)S(1)} async-done(((f32[8,3,1024]{2,1,0:T(4,128)}), f32[8,3,1024]{2,1,0:T(4,128)S(1)}, u32[]{:S(2)}, u32[]{:S(2)}) %all-to-all-start.4) | async-done | bytes 98336 | tf_op jit(solution)/shard_map/all_to_all | solution.py:16
  221.5 16.6 %all_to_all.38 = f32[64,1,65]{2,1,0:T(1,128)S(1)} all-to-all(f32[64,1,65]{2,1,0:T(1,128)S(1)} %broadcast_in_dim.35), channel_id=1, replica_groups=mesh['vertex'=64,'view'=8] {'vertex'}, dimensions={0} | all-to-all | bytes 33280 | tf_op jit(solution)/shard_map/all_to_all | solution.py:16
  (261 shorter events, 52.6 us)
Async XLA Ops:
  0.6 18.6 %copy-start = (bf16[64,3,1024]{2,0,1:T(8,128)(2,1)S(1)}, bf16[64,3,1024]{2,0,1:T(8,128)(2,1)}, u32[]{:S(2)}) copy-start(bf16[64,3,1024]{2,0,1:T(8,128)(2,1)} %param.17) | copy-start | bytes 1179652
  2.1 28.0 %all-to-all-start.1 = ((s32[1,64,4]{2,0,1:T(1,128)}), s32[1,64,4]{2,0,1:T(1,128)S(1)}, u32[]{:S(2)}, u32[]{:S(2)}) async-start(s32[1,64,4]{2,0,1:T(1,128)} %copy.71), calls=%async_computation.1 | async-start | bytes 65536 | tf_op jit(solution)/shard_map/all_to_all | solution.py:179
  30.7 11.7 %all-to-all-start = ((f32[8,3,1024]{2,1,0:T(4,128)}), f32[8,3,1024]{2,1,0:T(4,128)S(1)}, u32[]{:S(2)}, u32[]{:S(2)}) async-start(f32[8,3,1024]{2,1,0:T(4,128)} %broadcast_in_dim.32), calls=%async_computation | async-start | bytes 262144 | tf_op jit(solution)/shard_map/all_to_all | solution.py:16
  52.9 6.5 %copy-start.6 = (s32[32,8]{0,1:T(8,128)S(1)}, s32[32,8]{0,1:T(8,128)}, u32[]{:S(2)}) copy-start(s32[32,8]{0,1:T(8,128)} %param.21) | copy-start | bytes 3076
  52.9 6.6 %copy-start.5 = (f32[32,12]{0,1:T(8,128)S(1)}, f32[32,12]{0,1:T(8,128)}, u32[]{:S(2)}) copy-start(f32[32,12]{0,1:T(8,128)} %param.24) | copy-start | bytes 4612
  52.9 6.7 %copy-start.3 = (s32[32,256]{1,0:T(8,128)S(1)}, s32[32,256]{1,0:T(8,128)}, u32[]{:S(2)}) copy-start(s32[32,256]{1,0:T(8,128)} %param.22) | copy-start | bytes 98308
  52.9 6.7 %copy-start.2 = (f32[32,3,256]{2,0,1:T(8,128)S(1)}, f32[32,3,256]{2,0,1:T(8,128)}, u32[]{:S(2)}) copy-start(f32[32,3,256]{2,0,1:T(8,128)} %param.23) | copy-start | bytes 294916
  52.9 6.7 %copy-start.1 = (f32[32,3,256]{2,0,1:T(8,128)S(1)}, f32[32,3,256]{2,0,1:T(8,128)}, u32[]{:S(2)}) copy-start(f32[32,3,256]{2,0,1:T(8,128)} %param.25) | copy-start | bytes 294916
  54.7 35.4 %all-to-all-start.2 = ((f32[9,64,4,128]{3,2,0,1:T(4,128)}), f32[9,64,4,128]{3,2,0,1:T(4,128)S(1)}, u32[]{:S(2)}, u32[]{:S(2)}) async-start(f32[9,64,4,128]{3,2,0,1:T(4,128)} %copy.73), calls=%async_computation.2 | async-start | bytes 2359296 | tf_op jit(solution)/shard_map/all_to_all | solution.py:182
  153.5 36.3 %all-to-all-start.3 = ((f32[9,64,4,128]{3,2,0,1:T(4,128)}), f32[9,64,4,128]{3,2,0,1:T(4,128)S(1)}, u32[]{:S(2)}, u32[]{:S(2)}) async-start(f32[9,64,4,128]{3,2,0,1:T(4,128)} %copy.83), calls=%async_computation.3 | async-start | bytes 2359296 | tf_op jit(solution)/shard_map/all_to_all | solution.py:195
  191.0 18.5 %all-to-all-start.5 = ((f32[8,1,1]{2,1,0:T(1,128)}), f32[8,1,1]{2,1,0:T(1,128)S(1)}, u32[]{:S(2)}, u32[]{:S(2)}) async-start(f32[8,1,1]{2,1,0:T(1,128)} %broadcast_in_dim.34), calls=%async_computation.5 | async-start | bytes 8192 | tf_op jit(solution)/shard_map/all_to_all | solution.py:16
  210.2 10.1 %all-to-all-start.4 = ((f32[8,3,1024]{2,1,0:T(4,128)}), f32[8,3,1024]{2,1,0:T(4,128)S(1)}, u32[]{:S(2)}, u32[]{:S(2)}) async-start(f32[8,3,1024]{2,1,0:T(4,128)} %broadcast_in_dim.33), calls=%async_computation.4 | async-start | bytes 262144 | tf_op jit(solution)/shard_map/all_to_all | solution.py:16
  220.3 19.1 %copy-start.4 = (f32[3,1024]{1,0:T(4,128)}, f32[3,1024]{1,0:T(4,128)S(1)}, u32[]{:S(2)}) copy-start(f32[3,1024]{1,0:T(4,128)S(1)} %reduce_sum.82) | copy-start | bytes 36868
  238.1 1.2 copy-start.7
where the time goes:
time: 242 us; the launch traced here: 241 us
  waiting for transfers between devices  76.7 us (32%)
  matrix products  55.6 us (23%)
  starting transfers between devices  48.9 us (20%)
  local copies, waits for them, and re-layouts  28.8 us (12%)
  blocking collectives  16.6 us (7%)
  other arithmetic  10.2 us (4%)
  between operations  2.75 us (1%)
    all_to_all x1, waiting for transfers between devices, per_device(): lax.all_to_all(jnp.einsum('...b,dbl->d...l', onehot, corner_data, precisi...  30.2 us
    all_to_all x1, waiting for transfers between devices, per_device(): lax.all_to_all(grad_back, 'vertex', split_axis=1, concat_axis=1, tiled=True)  26.7 us
    dot_general x8, matrix products, shade_group(): jnp.einsum('gdp,gqp->gdq', grad_corner, onehot, precision=lax.Precision.H...  21.5 us
    all_to_all x3, starting transfers between devices, copy_for_each(): lax.all_to_all(jnp.broadcast_to(array[None], (size, *array.shape)), axis,...  19.5 us
    dot_general x8, matrix products, shade_group(): jnp.einsum('gdq,gqp->gdp', rows, onehot, precision=lax.Precision.HIGHEST)  18.9 us
    all_to_all x1, starting transfers between devices, per_device(): lax.all_to_all(fetch_list, 'vertex', split_axis=1, concat_axis=1, tiled=T...  17.1 us
    all_to_all x1, blocking collectives, copy_for_each(): lax.all_to_all(jnp.broadcast_to(array[None], (size, *array.shape)), axis,...  16.6 us
    all_to_all x1, waiting for transfers between devices, per_device(): lax.all_to_all(fetch_list, 'vertex', split_axis=1, concat_axis=1, tiled=T...  10 us
  transfers between devices with their start and end apart: 6, of which 5 were waited for; matrix products, arithmetic and copies ran while one was open for 6% of the time, Pallas kernels for 0%

commit v1 on v0

v1 whole, which is shorter than its diff:
```python
import jax
import jax.numpy as jnp
from jax import lax
from jax.experimental import pallas as pl
from jax.experimental.pallas import tpu as pltpu
from jax.sharding import PartitionSpec as P

LANES = 128
SMOOTH = 0.1
HOLDERS = 64
VIEWS = 8
OFFSETS = (-3, -2, -1, 0, 1, 2, 3, 32)
WIN = len(OFFSETS)
CAP = 4
COVER = 8
TILES = 32
ROW = 9 * LANES

F32 = jnp.float32
BF16 = jnp.bfloat16
VMEM = pl.BlockSpec(memory_space=pltpu.VMEM)
SMEM = pl.BlockSpec(memory_space=pltpu.SMEM)


def holder_of(u, slot):
    return (u + OFFSETS[slot]) & (HOLDERS - 1)


def owner_of(h, slot):
    return (h - OFFSETS[slot]) & (HOLDERS - 1)


def partial_kernel(coeff_ref, basis_ref, out_ref):
    total = jnp.zeros(basis_ref.shape[1:], F32)
    for k in range(basis_ref.shape[0]):
        total = total + coeff_ref[k] * basis_ref[k].astype(F32)
    for v in range(VIEWS):
        out_ref[v] = total[:, v * LANES : (v + 1) * LANES]


def holder_kernel(parts_ref, rest_ref, corner_ref, out_ref):
    position = rest_ref[...]
    for v in range(VIEWS):
        position = position + parts_ref[v]
    for row in range(9):
        value = position[row : row + 1] if row < 3 else corner_ref[row - 3 : row - 2]
        out_ref[:, :, row * LANES : (row + 1) * LANES] = jnp.broadcast_to(
            value[None], (HOLDERS, 1, LANES)
        )


def window_kernel(u_ref, slices_ref, out_ref):
    u = u_ref[0]
    for slot in range(WIN):
        value = slices_ref[pl.ds(holder_of(u, slot), 1)]
        out_ref[:, :, slot * ROW : (slot + 1) * ROW] = jnp.broadcast_to(value, (VIEWS, 1, ROW))


def pick_lanes(source, lane):
    return jnp.take_along_axis(source, lane, axis=1, mode="promise_in_bounds")


def high_low(values):
    high = values.astype(BF16).astype(F32)
    return jnp.concatenate([high, values - high], axis=0).astype(BF16)


def lane_onehot(lane_row):
    ids = lax.broadcasted_iota(jnp.int32, (LANES, LANES), 0)
    return jnp.where(ids == lane_row, 1.0, 0.0).astype(BF16)


def dot_nt(a, b):
    return lax.dot_general(a, b, (((1,), (1,)), ((), ())), preferred_element_type=F32)


def tile_kernel(
    block_ref,
    entry_ref,
    entry_row_ref,
    table_ref,
    slot_ref,
    weight_ref,
    camera_ref,
    target_ref,
    out_ref,
    energy_ref,
    slot_rows,
    corner_id,
    entry_table,
    corner_pix,
    grad_pix,
    tile_grad,
    entry_grad,
):
    sub8 = lax.broadcasted_iota(jnp.int32, (8, LANES), 0)
    for half in range(2):
        slot_rows[half * TILES : (half + 1) * TILES, :] = slot_ref[
            :, half * LANES : (half + 1) * LANES
        ]
    for j in range(WIN):
        for s in range(CAP):
            block = block_ref[j, s]
            for c in range(3):
                at = pl.multiple_of(
                    j * ROW + 3 * LANES + (2 * c + (block & 1)) * LANES, LANES
                )
                ids = table_ref[pl.ds(block >> 1, 1), 0, pl.ds(at, LANES)]
                corner_id[pl.ds(j * 16 + c * CAP + s, 1), :] = ids.astype(jnp.int32)
    for j in range(WIN):
        ids = [corner_id[pl.ds(j * 16 + 8 * i, 8), :] for i in range(2)]
        lane = [i & (LANES - 1) for i in ids]
        sub = [i >> 7 for i in ids]
        for d in range(3):
            at = j * ROW + d * LANES
            found = [jnp.zeros((8, LANES), F32)] * 2
            for s in range(8):
                source = jnp.broadcast_to(table_ref[s, :, at : at + LANES], (8, LANES))
                for i in range(2):
                    found[i] = jnp.where(sub[i] == s, pick_lanes(source, lane[i]), found[i])
            for c in range(3):
                rows = found[c // 2][(c % 2) * CAP : (c % 2) * CAP + CAP]
                entry_table[pl.ds(j * 64 + 3 * c + d, CAP, stride=16), :] = rows

    def gather_tile(t, carry):
        for half in range(2):
            q = slot_rows[pl.ds(half * TILES + t, 1), :]
            q = jnp.broadcast_to(q, (8, LANES))
            lane = q & (LANES - 1)
            which = q >> 7
            first = jnp.zeros((8, LANES), F32)
            second = jnp.zeros((8, LANES), F32)
            for n in range(COVER):
                at = pl.multiple_of(entry_ref[t, n] * 16, 16)
                mine = which == n
                first = jnp.where(mine, pick_lanes(entry_table[pl.ds(at, 8), :], lane), first)
                second = jnp.where(
                    mine, pick_lanes(entry_table[pl.ds(at + 8, 8), :], lane), second
                )
            row = half * TILES + t
            corner_pix[pl.ds(row, 8, stride=2 * TILES), :] = first
            corner_pix[pl.ds(8 * 2 * TILES + row, 1), :] = second[0:1]
        return carry

    lax.fori_loop(0, TILES, gather_tile, 0, unroll=2)

    energy = jnp.zeros((TILES, LANES), F32)
    for half in range(2):
        cols = slice(half * LANES, (half + 1) * LANES)
        weights = [weight_ref[:, c, cols] for c in range(3)]

        def rows_of(cd):
            return pl.ds(cd * 2 * TILES + half * TILES, TILES)

        surface = []
        for d in range(3):
            value = weights[0] * corner_pix[rows_of(d), :]
            value = value + weights[1] * corner_pix[rows_of(3 + d), :]
            surface.append(value + weights[2] * corner_pix[rows_of(6 + d), :])
        grad_surface = [jnp.zeros((TILES, LANES), F32)] * 3
        for r in range(3):
            linear = camera_ref[:, 3 * r : 3 * r + 1] * surface[0]
            linear = linear + camera_ref[:, 3 * r + 1 : 3 * r + 2] * surface[1]
            linear = linear + camera_ref[:, 3 * r + 2 : 3 * r + 3] * surface[2]
            shaded = jnp.tanh(linear + camera_ref[:, 9 + r : 10 + r])
            differ = shaded - target_ref[:, r, cols]
            spread = jnp.sqrt(differ * differ + SMOOTH * SMOOTH)
            energy = energy + spread
            grad_linear = differ / spread * (1.0 - shaded * shaded)
            for d in range(3):
                grad_surface[d] = (
                    grad_surface[d] + camera_ref[:, 3 * r + d : 3 * r + d + 1] * grad_linear
                )
        for c in range(3):
            for d in range(3):
                grad_pix[rows_of(3 * c + d), :] = weights[c] * grad_surface[d]
    energy_ref[...] = jnp.sum(energy, axis=0, keepdims=True)

    def scatter_tile(t, carry):
        spread_rows = [[] for _ in range(9)]
        onehot = []
        for half in range(2):
            q = slot_rows[pl.ds(half * TILES + t, 1), :]
            mine = jnp.broadcast_to(q >> 7, (8, LANES)) == sub8
            onehot.append(lane_onehot(jnp.broadcast_to(q & (LANES - 1), (LANES, LANES))))
            for cd in range(9):
                grad = grad_pix[pl.ds(cd * 2 * TILES + half * TILES + t, 1), :]
                grad = jnp.broadcast_to(grad, (8, LANES))
                spread_rows[cd].append(jnp.where(mine, grad, 0.0))
        rows = jnp.concatenate([jnp.concatenate(r, axis=1) for r in spread_rows], axis=0)
        summed = dot_nt(high_low(rows), jnp.concatenate(onehot, axis=1))
        summed = summed[:72] + summed[72:]
        at = pl.multiple_of(t * 8, 8)
        for cd in range(9):
            tile_grad[pl.ds(at, 8), cd * LANES : (cd + 1) * LANES] = summed[8 * cd : 8 * cd + 8]
        return carry

    lax.fori_loop(0, TILES, scatter_tile, 0, unroll=2)

    entry_ids = lax.broadcasted_iota(jnp.int32, (WIN * CAP, TILES * COVER), 0)
    pick = jnp.where(entry_ids == entry_row_ref[...], 1.0, 0.0).astype(BF16)
    values = tile_grad[...]
    high = values.astype(BF16)
    low = (values - high.astype(F32)).astype(BF16)
    entry_grad[...] = jnp.dot(pick, high, preferred_element_type=F32) + jnp.dot(
        pick, low, preferred_element_type=F32
    )

    for j in range(WIN):
        rows = [[] for _ in range(3)]
        onehot = []
        for c in range(3):
            for s in range(CAP):
                ids = corner_id[pl.ds(j * 16 + c * CAP + s, 1), :]
                mine = jnp.broadcast_to(ids >> 7, (8, LANES)) == sub8
                onehot.append(
                    lane_onehot(jnp.broadcast_to(ids & (LANES - 1), (LANES, LANES)))
                )
                for d in range(3):
                    at = (3 * c + d) * LANES
                    grad = entry_grad[pl.ds(j * CAP + s, 1), at : at + LANES]
                    rows[d].append(jnp.where(mine, jnp.broadcast_to(grad, (8, LANES)), 0.0))
        stacked = jnp.concatenate([jnp.concatenate(r, axis=1) for r in rows], axis=0)
        summed = dot_nt(high_low(stacked), jnp.concatenate(onehot, axis=1))
        for d in range(3):
            out_ref[:, j * 3 + d, :] = summed[8 * d : 8 * d + 8] + summed[24 + 8 * d : 32 + 8 * d]


def owner_sum_kernel(u_ref, parts_ref, out_ref):
    u = u_ref[0]
    total = parts_ref[0]
    for v in range(1, VIEWS):
        total = total + parts_ref[v]
    out_ref[...] = jnp.zeros(out_ref.shape, F32)
    for slot in range(WIN):
        for d in range(3):
            row = slot * 3 + d
            out_ref[pl.ds(holder_of(u, slot), 1), :, d * LANES : (d + 1) * LANES] = total[
                row : row + 1
            ][None]


def holder_sum_kernel(u_ref, parts_ref, energy_ref, out_ref):
    h = u_ref[0]
    total = parts_ref[pl.ds(owner_of(h, 0), 1)]
    for slot in range(1, WIN):
        total = total + parts_ref[pl.ds(owner_of(h, slot), 1)]
    out_ref[:, :, : 3 * LANES] = jnp.broadcast_to(total, (VIEWS, 1, 3 * LANES))
    out_ref[:, :, 3 * LANES :] = jnp.broadcast_to(energy_ref[...][None], (VIEWS, 1, LANES))


def project_kernel(slices_ref, basis_ref, grad_ref, out_ref):
    shapes = basis_ref.shape[0]
    total = jnp.zeros((shapes, 3, LANES), F32)
    energy = jnp.zeros((1, LANES), F32)
    for v in range(VIEWS):
        cols = slice(v * LANES, (v + 1) * LANES)
        for d in range(3):
            grad_ref[d : d + 1, cols] = slices_ref[v, :, d * LANES : (d + 1) * LANES]
        energy = energy + slices_ref[v, :, 3 * LANES :]
        total = total + basis_ref[:, :, cols].astype(F32) * grad_ref[:, cols][None]
    lanes = jnp.sum(total, axis=1)
    row = lax.dot_general(
        jnp.ones((8, LANES), F32),
        lanes,
        (((1,), (1,)), ((), ())),
        precision=lax.Precision.HIGHEST,
        preferred_element_type=F32,
    )[0:1]
    row = jnp.concatenate([row, jnp.zeros((1, LANES - shapes), F32)], axis=1)
    out_ref[:, :, :LANES] = jnp.broadcast_to(row[None], (HOLDERS, 1, LANES))
    out_ref[:, :, LANES:] = jnp.broadcast_to(energy[None], (HOLDERS, 1, LANES))


def call(kernel, out_shapes, args, scalars=0, scratch=(), name=None):
    shapes = [jax.ShapeDtypeStruct(s, F32) for s in out_shapes]
    single = len(shapes) == 1
    return pl.pallas_call(
        kernel,
        out_shape=shapes[0] if single else shapes,
        in_specs=[SMEM] * scalars + [VMEM] * (len(args) - scalars),
        out_specs=VMEM if single else [VMEM] * len(shapes),
        scratch_shapes=list(scratch),
        name=name,
    )(*args)


def exchange(array, axis):
    return lax.all_to_all(array, axis, 0, 0, tiled=True)


def tile_call(block_ids, entries, table, pix_slot, barycentric, camera, target):
    return call(
        tile_kernel,
        [(VIEWS, 3 * WIN, LANES), (1, LANES)],
        (
            block_ids,
            entries,
            entries.reshape(1, TILES * COVER),
            table,
            pix_slot,
            barycentric,
            camera,
            target,
        ),
        scalars=2,
        scratch=(
            pltpu.VMEM((2 * TILES, LANES), jnp.int32),
            pltpu.VMEM((16 * WIN, LANES), jnp.int32),
            pltpu.VMEM((16 * WIN * CAP, LANES), F32),
            pltpu.VMEM((9 * 2 * TILES, LANES), F32),
            pltpu.VMEM((9 * 2 * TILES, LANES), F32),
            pltpu.VMEM((TILES * COVER, 9 * LANES), F32),
            pltpu.VMEM((WIN * CAP, 9 * LANES), F32),
        ),
        name="tiles",
    )


def own_requests(u, fetch_list, tile_cover):
    doubled = jnp.concatenate([fetch_list[0], fetch_list[0]], axis=0)
    near = lax.dynamic_slice(doubled, ((u - 3) & (HOLDERS - 1), 0), (WIN - 1, CAP))
    far = lax.dynamic_slice(doubled, ((u + 32) & (HOLDERS - 1), 0), (1, CAP))
    block_ids = jnp.maximum(jnp.concatenate([near, far], axis=0), 0)
    relative = ((tile_cover >> 2) - u + 3) & (HOLDERS - 1)
    entries = jnp.minimum(relative, WIN - 1) * CAP + (tile_cover & (CAP - 1))
    return block_ids, entries


def per_device(
    coeffs,
    shape_basis,
    rest_pose,
    triangles,
    fetch_list,
    tile_cover,
    pix_slot,
    barycentric,
    camera,
    target,
):
    u = lax.axis_index("vertex").astype(jnp.int32)
    view = lax.axis_index("view").astype(jnp.int32)
    u_array = u.reshape(1)
    pixels = (
        tile_cover.shape[0] * pix_slot.shape[1] * lax.axis_size("vertex") * lax.axis_size("view")
    )

    partial = call(
        partial_kernel,
        [(VIEWS, 3, LANES)],
        (coeffs.astype(F32), shape_basis),
        scalars=1,
        name="offsets",
    )
    parts = exchange(partial, "view")
    rest = lax.dynamic_slice(rest_pose, (0, view * LANES), (3, LANES))
    corners = lax.dynamic_slice(triangles, (0, view * 2 * LANES), (3, 2 * LANES))
    corners = corners.reshape(6, LANES).astype(F32)
    slices = call(
        holder_kernel, [(HOLDERS, 1, ROW)], (parts, rest, corners), name="holder"
    )
    slices = exchange(slices, "vertex")
    table = call(
        window_kernel, [(VIEWS, 1, WIN * ROW)], (u_array, slices), scalars=1, name="window"
    )
    table = exchange(table, "view")

    block_ids, entries = own_requests(u, fetch_list, tile_cover)
    parts, energy = tile_call(
        block_ids, entries, table, pix_slot, barycentric, camera, target
    )

    parts = exchange(parts, "view")
    parts = call(
        owner_sum_kernel, [(HOLDERS, 1, 3 * LANES)], (u_array, parts), scalars=1, name="owner_sum"
    )
    parts = exchange(parts, "vertex")
    slices = call(
        holder_sum_kernel,
        [(VIEWS, 1, 4 * LANES)],
        (u_array, parts, energy),
        scalars=1,
        name="holder_sum",
    )
    slices = exchange(slices, "view")
    vertex_grad, rows = call(
        project_kernel,
        [(3, VIEWS * LANES), (HOLDERS, 1, 2 * LANES)],
        (slices, shape_basis),
        name="project",
    )
    total = exchange(rows, "vertex").sum(axis=(0, 1))
    coeff_grad = total[: coeffs.shape[0]]
    energy = jnp.sum(total[LANES:])
    return (energy / pixels, vertex_grad, coeff_grad)


def solution(mesh):
    placed = (
        P("view"),
        P("view", None, "vertex"),
        P(None, "vertex"),
        P(None, "vertex"),
        P(("vertex", "view"), None, None),
        P(("vertex", "view"), None),
        P(("vertex", "view"), None),
        P(("vertex", "view"), None, None),
        P(("vertex", "view"), None),
        P(("vertex", "view"), None, None),
    )
    return jax.shard_map(
        per_device,
        mesh=mesh,
        in_specs=placed,
        out_specs=(P(), P(None, "vertex"), P("view")),
        check_vma=False,
    )
```

time: 242 us -> 136 us (0.56)
  waiting for transfers between devices: 76.7 us -> 17.5 us
  matrix products: 55.6 us -> 0 us
  blocking collectives: 16.6 us -> 53 us
  Pallas kernels: 0 us -> 20.5 us
  starting transfers between devices: 48.9 us -> 28.8 us
  local copies, waits for them, and re-layouts: 28.8 us -> 10.5 us
  other arithmetic: 10.2 us -> 2.58 us
    all_to_all x6 -> x3, waiting for transfers between devices: 76.7 us -> 17.5 us  [exchange(): return lax.all_to_all(array, axis, 0, 0, tiled=True)]
    dot_general x46 -> x0, matrix products: 55.6 us -> none  [the longest x8 21.5 us: shade_group(): jnp.einsum('gdp,gqp->gdq', grad_corner, onehot, precision=lax.Precision.H...]
    all_to_all x1 -> x4, blocking collectives: 16.6 us -> 53 us  [exchange(): return lax.all_to_all(array, axis, 0, 0, tiled=True)]
    pallas_call x0 -> x7, Pallas kernels: none -> 20.5 us  [call(): pl.pallas_call(kernel, out_shape=shapes[0] if single else shapes, in_spec...]
    all_to_all x6 -> x3, starting transfers between devices: 48.9 us -> 28.8 us  [exchange(): return lax.all_to_all(array, axis, 0, 0, tiled=True)]
    slice x33 -> x1, local copies, waits for them, and re-layouts: 9.02 us -> 0.51 us  [per_device(): coeff_grad = total[:coeffs.shape[0]]]
    reduce_sum x13 -> x2, other arithmetic: 6.99 us -> 0.7 us  [the longest x1 0.6 us: per_device(): energy = jnp.sum(total[LANES:])]
    unnamed x20 -> x29, local copies, waits for them, and re-layouts: 1.7 us -> 7.99 us
  transfers between devices with their start and end apart: 6 -> 3, of which waited for: 5 -> 3; matrix products, arithmetic and copies ran while one was open for 6% -> 4% of each run, Pallas kernels for 0% -> 0%
where the time goes in v1:
time: 136 us; the launch traced here: 135 us
  blocking collectives  53 us (39%)
  starting transfers between devices  28.8 us (21%)
  Pallas kernels  20.5 us (15%)
  waiting for transfers between devices  17.5 us (13%)
  local copies, waits for them, and re-layouts  10.5 us (8%)
  other arithmetic  2.58 us (2%)
  between operations  2.49 us (2%)
    all_to_all x4, blocking collectives, exchange(): return lax.all_to_all(array, axis, 0, 0, tiled=True)  53 us
    all_to_all x3, starting transfers between devices, exchange(): return lax.all_to_all(array, axis, 0, 0, tiled=True)  28.8 us
    pallas_call x7, Pallas kernels, call(): pl.pallas_call(kernel, out_shape=shapes[0] if single else shapes, in_spec...  20.5 us
    all_to_all x3, waiting for transfers between devices, exchange(): return lax.all_to_all(array, axis, 0, 0, tiled=True)  17.5 us
    unnamed x29, local copies, waits for them, and re-layouts  7.99 us
  transfers between devices with their start and end apart: 3, of which 3 were waited for; matrix products, arithmetic and copies ran while one was open for 4% of the time, Pallas kernels for 0%

profile of v1, /device:TPU:1, one launch (start us, length us, event | category | flops | bytes accessed | tf_op | source)
XLA Modules:
  0.0 135.4 jit_solution(9363412871095524185)
XLA Ops:
  0.7 2.1 %copy.43.basis_ref = bf16[64,3,1024]{2,1,0:T(4,128)(2,1)} copy(bf16[64,3,1024]{2,0,1:T(8,128)(2,1)} %param.11) | data formatting | bytes 786432 | tf_op args[1]
  3.3 1.8 %offsets.1 = f32[8,3,128]{2,1,0:T(4,128)} custom-call(f32[64]{0:T(128)} %convert_element_type.8.coeff_ref, bf16[64,3,1024]{2,1,0:T(4,128)(2,1)} %copy.43.basis_ref), custom_call_target="tpu_custom_call" | custom-call | tf_op jit(solution)/shard_map/offsets/pallas_call | solution.py:278
  5.1 10.1 %all-to-all-start = ((f32[8,3,128]{2,1,0:T(4,128)}), f32[8,3,128]{2,1,0:T(4,128)S(1)}, u32[]{:S(2)}, u32[]{:S(2)}) async-start(f32[8,3,128]{2,1,0:T(4,128)} %offsets.1), calls=%async_computation | async-start | bytes 32768 | tf_op jit(solution)/shard_map/all_to_all | solution.py:289
  15.2 0.7 dynamic-slice_convert_fusion
  15.9 0.6 constant_dynamic-slice_fusion.rest_ref
  16.5 0.6 convert_element_type.10.corner_ref
  17.1 2.8 %all-to-all-done.parts_ref = f32[8,3,128]{2,1,0:T(4,128)S(1)} async-done(((f32[8,3,128]{2,1,0:T(4,128)}), f32[8,3,128]{2,1,0:T(4,128)S(1)}, u32[]{:S(2)}, u32[]{:S(2)}) %all-to-all-start) | async-done | bytes 12320 | tf_op jit(solution)/shard_map/all_to_all | solution.py:289
  19.9 0.6 copy-done.6
  20.5 1.6 %holder.1 = f32[64,1,1152]{2,1,0:T(1,128)} custom-call(f32[8,3,128]{2,1,0:T(4,128)} %copy-done.6, f32[3,128]{1,0:T(4,128)} %constant_dynamic-slice_fusion.rest_ref, f32[6,128]{1,0:T(8,128)} %convert_element_type.10.corner_ref), custom_call_target="tpu_custom_call" | custom-call | tf_op jit(solution)/shard_map/holder/pallas_call | solution.py:278
  22.1 12.0 %all-to-all-start.1 = ((f32[64,1,1152]{2,1,0:T(1,128)}), f32[64,1,1152]{2,1,0:T(1,128)S(1)}, u32[]{:S(2)}, u32[]{:S(2)}) async-start(f32[64,1,1152]{2,1,0:T(1,128)} %holder.1), calls=%async_computation.1 | async-start | bytes 589824 | tf_op jit(solution)/shard_map/all_to_all | solution.py:289
  34.1 0.7 copy-done.9
  35.2 0.5 copy-done.8
  35.8 11.5 %all-to-all-done.1.slices_ref = f32[64,1,1152]{2,1,0:T(1,128)S(1)} async-done(((f32[64,1,1152]{2,1,0:T(1,128)}), f32[64,1,1152]{2,1,0:T(1,128)S(1)}, u32[]{:S(2)}, u32[]{:S(2)}) %all-to-all-start.1) | async-done | bytes 294944 | tf_op jit(solution)/shard_map/all_to_all | solution.py:289
  47.3 0.7 copy-done.2
  48.0 1.7 %window.1 = f32[8,1,9216]{2,1,0:T(1,128)} custom-call(s32[1]{0:T(128)} %bitcast.u_ref, f32[64,1,1152]{2,1,0:T(1,128)} %copy-done.2), custom_call_target="tpu_custom_call" | custom-call | tf_op jit(solution)/shard_map/window/pallas_call | solution.py:278
  49.8 6.7 %all-to-all-start.2 = ((f32[8,1,9216]{2,1,0:T(1,128)}), f32[8,1,9216]{2,1,0:T(1,128)S(1)}, u32[]{:S(2)}, u32[]{:S(2)}) async-start(f32[8,1,9216]{2,1,0:T(1,128)} %window.1), calls=%async_computation.2 | async-start | bytes 589824 | tf_op jit(solution)/shard_map/all_to_all | solution.py:289
  56.5 0.7 reshape.15.entry_row_ref
  57.2 0.7 copy.44.weight_ref
  58.1 0.7 copy.46.target_ref
  58.8 0.7 copy.45.camera_ref
  59.5 0.6 add_maximum_fusion.block_ref
  60.1 3.2 %all-to-all-done.2.table_ref = f32[8,1,9216]{2,1,0:T(1,128)S(1)} async-done(((f32[8,1,9216]{2,1,0:T(1,128)}), f32[8,1,9216]{2,1,0:T(1,128)S(1)}, u32[]{:S(2)}, u32[]{:S(2)}) %all-to-all-start.2) | async-done | bytes 294944 | tf_op jit(solution)/shard_map/all_to_all | solution.py:289
  63.3 0.7 copy-done.1
  64.0 10.2 %tiles.1 = (f32[8,24,128]{2,1,0:T(8,128)}, f32[1,128]{1,0:T(1,128)}) custom-call(s32[8,4]{1,0:T(8,128)} %add_maximum_fusion.block_ref, s32[32,8]{1,0:T(8,128)} %copy-done.3, s32[1,256]{1,0:T(1,128)} %reshape.15.entry_row_ref, f32[8,1,9216]{2,1,0:T(1,128)} %copy-done.1, s32[32,256]{1,0:T(8,128)} %slot_ref.1, f32[32,3,256]{2,1,0:T(4,128)} %copy.44.weight_ref, ...), custom_call_target="tpu_custom_call" | custom-call | tf_op jit(solution)/shard_map/tiles/pallas_call | solution.py:278
  74.2 10.0 %all_to_all.35.parts_ref = f32[8,24,128]{2,1,0:T(8,128)} all-to-all(f32[8,24,128]{2,1,0:T(8,128)} %get-tuple-element.7), channel_id=1, replica_groups=mesh['vertex'=64,'view'=8] {'view'}, dimensions={0} | all-to-all | bytes 196608 | tf_op jit(solution)/shard_map/all_to_all | solution.py:289
  84.3 1.5 %owner_sum.1 = f32[64,1,384]{2,1,0:T(1,128)} custom-call(s32[1]{0:T(128)} %bitcast.u_ref, f32[8,24,128]{2,1,0:T(8,128)} %all_to_all.35.parts_ref), custom_call_target="tpu_custom_call" | custom-call | tf_op jit(solution)/shard_map/owner_sum/pallas_call | solution.py:278
  85.8 16.6 %all_to_all.36.parts_ref = f32[64,1,384]{2,1,0:T(1,128)} all-to-all(f32[64,1,384]{2,1,0:T(1,128)} %owner_sum.1), channel_id=1, replica_groups=mesh['vertex'=64,'view'=8] {'vertex'}, dimensions={0} | all-to-all | bytes 196608 | tf_op jit(solution)/shard_map/all_to_all | solution.py:289
  102.5 1.5 %holder_sum.1 = f32[8,1,512]{2,1,0:T(1,128)} custom-call(s32[1]{0:T(128)} %bitcast.u_ref, f32[64,1,384]{2,1,0:T(1,128)} %all_to_all.36.parts_ref, f32[1,128]{1,0:T(1,128)} %get-tuple-element.8.energy_ref), custom_call_target="tpu_custom_call" | custom-call | tf_op jit(solution)/shard_map/holder_sum/pallas_call | solution.py:278
  104.0 10.5 %all_to_all.37.slices_ref = f32[8,1,512]{2,1,0:T(1,128)} all-to-all(f32[8,1,512]{2,1,0:T(1,128)} %holder_sum.1), channel_id=1, replica_groups=mesh['vertex'=64,'view'=8] {'view'}, dimensions={0} | all-to-all | bytes 32768 | tf_op jit(solution)/shard_map/all_to_all | solution.py:289
  114.5 2.1 %project.1 = (f32[3,1024]{1,0:T(4,128)}, f32[64,1,256]{2,1,0:T(1,128)}) custom-call(f32[8,1,512]{2,1,0:T(1,128)} %all_to_all.37.slices_ref, bf16[64,3,1024]{2,1,0:T(4,128)(2,1)} %copy.43.basis_ref), custom_call_target="tpu_custom_call" | custom-call | tf_op jit(solution)/shard_map/project/pallas_call | solution.py:278
  116.6 15.8 %all_to_all.38 = f32[64,1,256]{2,1,0:T(1,128)S(1)} all-to-all(f32[64,1,256]{2,1,0:T(1,128)} %get-tuple-element.9), channel_id=1, replica_groups=mesh['vertex'=64,'view'=8] {'vertex'}, dimensions={0} | all-to-all | bytes 131072 | tf_op jit(solution)/shard_map/all_to_all | solution.py:289
  132.5 0.6 slice_reduce_fusion
  (27 shorter events, 1.8 us)
Async XLA Ops:
  0.6 15.3 %copy-start = (f32[3,1024]{1,0:T(4,128)S(1)}, f32[3,1024]{1,0:T(4,128)}, u32[]{:S(2)}) copy-start(f32[3,1024]{1,0:T(4,128)} %param.12) | copy-start | bytes 36868
  0.6 2.2 %copy-start.10 = (bf16[64]{0:T(256)(128)(2,1)S(1)}, bf16[64]{0:T(256)(128)(2,1)}, u32[]{:S(2)}) copy-start(bf16[64]{0:T(256)(128)(2,1)} %param.10) | copy-start | bytes 388
  5.1 14.7 %all-to-all-start = ((f32[8,3,128]{2,1,0:T(4,128)}), f32[8,3,128]{2,1,0:T(4,128)S(1)}, u32[]{:S(2)}, u32[]{:S(2)}) async-start(f32[8,3,128]{2,1,0:T(4,128)} %offsets.1), calls=%async_computation | async-start | bytes 32768 | tf_op jit(solution)/shard_map/all_to_all | solution.py:289
  19.9 0.6 copy-start.6
  22.1 25.2 %all-to-all-start.1 = ((f32[64,1,1152]{2,1,0:T(1,128)}), f32[64,1,1152]{2,1,0:T(1,128)S(1)}, u32[]{:S(2)}, u32[]{:S(2)}) async-start(f32[64,1,1152]{2,1,0:T(1,128)} %holder.1), calls=%async_computation.1 | async-start | bytes 589824 | tf_op jit(solution)/shard_map/all_to_all | solution.py:289
  34.1 0.7 copy-start.9
  35.0 0.7 copy-start.8
  47.3 0.7 copy-start.2
  49.8 7.4 %copy-start.4 = (f32[32,3,256]{2,0,1:T(8,128)S(1)}, f32[32,3,256]{2,0,1:T(8,128)}, u32[]{:S(2)}) copy-start(f32[32,3,256]{2,0,1:T(8,128)} %param.17) | copy-start | bytes 294916
  49.8 13.5 %all-to-all-start.2 = ((f32[8,1,9216]{2,1,0:T(1,128)}), f32[8,1,9216]{2,1,0:T(1,128)S(1)}, u32[]{:S(2)}, u32[]{:S(2)}) async-start(f32[8,1,9216]{2,1,0:T(1,128)} %window.1), calls=%async_computation.2 | async-start | bytes 589824 | tf_op jit(solution)/shard_map/all_to_all | solution.py:289
  56.5 1.4 %copy-start.3 = (s32[32,8]{1,0:T(8,128)}, s32[32,8]{1,0:T(8,128)S(1)}, u32[]{:S(2)}) copy-start(s32[32,8]{1,0:T(8,128)S(1)} %and_add_fusion.entry_ref) | copy-start | bytes 3076
  57.2 0.9 copy-start.5
  58.1 0.7 copy-start.7
  63.3 0.7 copy-start.1

commit v2 on v1

--- a/solution.py
+++ b/solution.py
@@ -7,53 +7,19 @@
 
 LANES = 128
 SMOOTH = 0.1
-HOLDERS = 64
 VIEWS = 8
 OFFSETS = (-3, -2, -1, 0, 1, 2, 3, 32)
 WIN = len(OFFSETS)
 CAP = 4
 COVER = 8
 TILES = 32
-ROW = 9 * LANES
+BLOCKS = 16
+SHARD = 24 + 3 * BLOCKS
 
 F32 = jnp.float32
 BF16 = jnp.bfloat16
 VMEM = pl.BlockSpec(memory_space=pltpu.VMEM)
 SMEM = pl.BlockSpec(memory_space=pltpu.SMEM)
-
-
-def holder_of(u, slot):
-    return (u + OFFSETS[slot]) & (HOLDERS - 1)
-
-
-def owner_of(h, slot):
-    return (h - OFFSETS[slot]) & (HOLDERS - 1)
-
-
-def partial_kernel(coeff_ref, basis_ref, out_ref):
-    total = jnp.zeros(basis_ref.shape[1:], F32)
-    for k in range(basis_ref.shape[0]):
-        total = total + coeff_ref[k] * basis_ref[k].astype(F32)
-    for v in range(VIEWS):
-        out_ref[v] = total[:, v * LANES : (v + 1) * LANES]
-
-
-def holder_kernel(parts_ref, rest_ref, corner_ref, out_ref):
-    position = rest_ref[...]
-    for v in range(VIEWS):
-        position = position + parts_ref[v]
-    for row in range(9):
-        value = position[row : row + 1] if row < 3 else corner_ref[row - 3 : row - 2]
-        out_ref[:, :, row * LANES : (row + 1) * LANES] = jnp.broadcast_to(
-            value[None], (HOLDERS, 1, LANES)
-        )
-
-
-def window_kernel(u_ref, slices_ref, out_ref):
-    u = u_ref[0]
-    for slot in range(WIN):
-        value = slices_ref[pl.ds(holder_of(u, slot), 1)]
-        out_ref[:, :, slot * ROW : (slot + 1) * ROW] = jnp.broadcast_to(value, (VIEWS, 1, ROW))
 
 
 def pick_lanes(source, lane):
@@ -102,20 +68,16 @@
         for s in range(CAP):
             block = block_ref[j, s]
             for c in range(3):
-                at = pl.multiple_of(
-                    j * ROW + 3 * LANES + (2 * c + (block & 1)) * LANES, LANES
-                )
-                ids = table_ref[pl.ds(block >> 1, 1), 0, pl.ds(at, LANES)]
+                ids = table_ref[j, pl.ds(24 + c * BLOCKS + block, 1), :]
                 corner_id[pl.ds(j * 16 + c * CAP + s, 1), :] = ids.astype(jnp.int32)
     for j in range(WIN):
         ids = [corner_id[pl.ds(j * 16 + 8 * i, 8), :] for i in range(2)]
         lane = [i & (LANES - 1) for i in ids]
         sub = [i >> 7 for i in ids]
         for d in range(3):
-            at = j * ROW + d * LANES
             found = [jnp.zeros((8, LANES), F32)] * 2
             for s in range(8):
-                source = jnp.broadcast_to(table_ref[s, :, at : at + LANES], (8, LANES))
+                source = jnp.broadcast_to(table_ref[j, 8 * d + s : 8 * d + s + 1, :], (8, LANES))
                 for i in range(2):
                     found[i] = jnp.where(sub[i] == s, pick_lanes(source, lane[i]), found[i])
             for c in range(3):
@@ -147,7 +109,7 @@
     energy = jnp.zeros((TILES, LANES), F32)
     for half in range(2):
         cols = slice(half * LANES, (half + 1) * LANES)
-        weights = [weight_ref[:, c, cols] for c in range(3)]
+        weights = [weight_ref[c, :, cols] for c in range(3)]
 
         def rows_of(cd):
             return pl.ds(cd * 2 * TILES + half * TILES, TILES)
@@ -163,7 +125,7 @@
             linear = linear + camera_ref[:, 3 * r + 1 : 3 * r + 2] * surface[1]
             linear = linear + camera_ref[:, 3 * r + 2 : 3 * r + 3] * surface[2]
             shaded = jnp.tanh(linear + camera_ref[:, 9 + r : 10 + r])
-            differ = shaded - target_ref[:, r, cols]
+            differ = shaded - target_ref[r, :, cols]
             spread = jnp.sqrt(differ * differ + SMOOTH * SMOOTH)
             energy = energy + spread
             grad_linear = differ / spread * (1.0 - shaded * shaded)
@@ -174,7 +136,7 @@
         for c in range(3):
             for d in range(3):
                 grad_pix[rows_of(3 * c + d), :] = weights[c] * grad_surface[d]
-    energy_ref[...] = jnp.sum(energy, axis=0, keepdims=True)
+    energy_ref[...] = energy[0:8] + energy[8:16] + energy[16:24] + energy[24:32]
 
     def scatter_tile(t, carry):
         spread_rows = [[] for _ in range(9)]
@@ -223,53 +185,9 @@
         stacked = jnp.concatenate([jnp.concatenate(r, axis=1) for r in rows], axis=0)
         summed = dot_nt(high_low(stacked), jnp.concatenate(onehot, axis=1))
         for d in range(3):
-            out_ref[:, j * 3 + d, :] = summed[8 * d : 8 * d + 8] + summed[24 + 8 * d : 32 + 8 * d]
-
-
-def owner_sum_kernel(u_ref, parts_ref, out_ref):
-    u = u_ref[0]
-    total = parts_ref[0]
-    for v in range(1, VIEWS):
-        total = total + parts_ref[v]
-    out_ref[...] = jnp.zeros(out_ref.shape, F32)
-    for slot in range(WIN):
-        for d in range(3):
-            row = slot * 3 + d
-            out_ref[pl.ds(holder_of(u, slot), 1), :, d * LANES : (d + 1) * LANES] = total[
-                row : row + 1
-            ][None]
-
-
-def holder_sum_kernel(u_ref, parts_ref, energy_ref, out_ref):
-    h = u_ref[0]
-    total = parts_ref[pl.ds(owner_of(h, 0), 1)]
-    for slot in range(1, WIN):
-        total = total + parts_ref[pl.ds(owner_of(h, slot), 1)]
-    out_ref[:, :, : 3 * LANES] = jnp.broadcast_to(total, (VIEWS, 1, 3 * LANES))
-    out_ref[:, :, 3 * LANES :] = jnp.broadcast_to(energy_ref[...][None], (VIEWS, 1, LANES))
-
-
-def project_kernel(slices_ref, basis_ref, grad_ref, out_ref):
-    shapes = basis_ref.shape[0]
-    total = jnp.zeros((shapes, 3, LANES), F32)
-    energy = jnp.zeros((1, LANES), F32)
-    for v in range(VIEWS):
-        cols = slice(v * LANES, (v + 1) * LANES)
-        for d in range(3):
-            grad_ref[d : d + 1, cols] = slices_ref[v, :, d * LANES : (d + 1) * LANES]
-        energy = energy + slices_ref[v, :, 3 * LANES :]
-        total = total + basis_ref[:, :, cols].astype(F32) * grad_ref[:, cols][None]
-    lanes = jnp.sum(total, axis=1)
-    row = lax.dot_general(
-        jnp.ones((8, LANES), F32),
-        lanes,
-        (((1,), (1,)), ((), ())),
-        precision=lax.Precision.HIGHEST,
-        preferred_element_type=F32,
-    )[0:1]
-    row = jnp.concatenate([row, jnp.zeros((1, LANES - shapes), F32)], axis=1)
-    out_ref[:, :, :LANES] = jnp.broadcast_to(row[None], (HOLDERS, 1, LANES))
-    out_ref[:, :, LANES:] = jnp.broadcast_to(energy[None], (HOLDERS, 1, LANES))
+            out_ref[j, 8 * d : 8 * d + 8, :] = (
+                summed[8 * d : 8 * d + 8] + summed[24 + 8 * d : 32 + 8 * d]
+            )
 
 
 def call(kernel, out_shapes, args, scalars=0, scratch=(), name=None):
@@ -292,7 +210,7 @@
 def tile_call(block_ids, entries, table, pix_slot, barycentric, camera, target):
     return call(
         tile_kernel,
-        [(VIEWS, 3 * WIN, LANES), (1, LANES)],
+        [(WIN, 24, LANES), (8, LANES)],
         (
             block_ids,
             entries,
@@ -318,13 +236,29 @@
 
 
 def own_requests(u, fetch_list, tile_cover):
+    holders = fetch_list.shape[1]
     doubled = jnp.concatenate([fetch_list[0], fetch_list[0]], axis=0)
-    near = lax.dynamic_slice(doubled, ((u - 3) & (HOLDERS - 1), 0), (WIN - 1, CAP))
-    far = lax.dynamic_slice(doubled, ((u + 32) & (HOLDERS - 1), 0), (1, CAP))
+    near = lax.dynamic_slice(doubled, ((u - 3) & (holders - 1), 0), (WIN - 1, CAP))
+    far = lax.dynamic_slice(doubled, ((u + 32) & (holders - 1), 0), (1, CAP))
     block_ids = jnp.maximum(jnp.concatenate([near, far], axis=0), 0)
-    relative = ((tile_cover >> 2) - u + 3) & (HOLDERS - 1)
+    relative = ((tile_cover >> 2) - u + 3) & (holders - 1)
     entries = jnp.minimum(relative, WIN - 1) * CAP + (tile_cover & (CAP - 1))
     return block_ids, entries
+
+
+def to_all(array, axis):
+    size = lax.axis_size(axis)
+    return exchange(jnp.broadcast_to(array[None], (size, *array.shape)), axis)
+
+
+def along_window(array, sign):
+    holders = lax.axis_size("vertex")
+    pairs = [
+        (h * VIEWS + j, (h + sign * OFFSETS[j]) % holders * VIEWS + j)
+        for h in range(holders)
+        for j in range(VIEWS)
+    ]
+    return lax.ppermute(array, ("vertex", "view"), pairs)
 
 
 def per_device(
@@ -340,60 +274,37 @@
     target,
 ):
     u = lax.axis_index("vertex").astype(jnp.int32)
-    view = lax.axis_index("view").astype(jnp.int32)
-    u_array = u.reshape(1)
     pixels = (
         tile_cover.shape[0] * pix_slot.shape[1] * lax.axis_size("vertex") * lax.axis_size("view")
     )
-
-    partial = call(
-        partial_kernel,
-        [(VIEWS, 3, LANES)],
-        (coeffs.astype(F32), shape_basis),
-        scalars=1,
-        name="offsets",
-    )
-    parts = exchange(partial, "view")
-    rest = lax.dynamic_slice(rest_pose, (0, view * LANES), (3, LANES))
-    corners = lax.dynamic_slice(triangles, (0, view * 2 * LANES), (3, 2 * LANES))
-    corners = corners.reshape(6, LANES).astype(F32)
-    slices = call(
-        holder_kernel, [(HOLDERS, 1, ROW)], (parts, rest, corners), name="holder"
-    )
-    slices = exchange(slices, "vertex")
-    table = call(
-        window_kernel, [(VIEWS, 1, WIN * ROW)], (u_array, slices), scalars=1, name="window"
-    )
-    table = exchange(table, "view")
-
+    shapes = coeffs.shape[0]
+    basis = jnp.transpose(shape_basis, (1, 0, 2))
+    corners = triangles.reshape(3 * BLOCKS, LANES).astype(F32)
     block_ids, entries = own_requests(u, fetch_list, tile_cover)
+
+    partial = jnp.sum(coeffs.astype(F32)[None, :, None] * basis.astype(F32), axis=1)
+    partial = lax.optimization_barrier(partial).reshape(24, LANES)
+    positions = rest_pose.reshape(24, LANES) + to_all(partial, "view").sum(axis=0)
+    shard = along_window(jnp.concatenate([positions, corners], axis=0), -1)
+    table = to_all(shard, "view")
     parts, energy = tile_call(
-        block_ids, entries, table, pix_slot, barycentric, camera, target
-    )
-
-    parts = exchange(parts, "view")
-    parts = call(
-        owner_sum_kernel, [(HOLDERS, 1, 3 * LANES)], (u_array, parts), scalars=1, name="owner_sum"
-    )
-    parts = exchange(parts, "vertex")
-    slices = call(
-        holder_sum_kernel,
-        [(VIEWS, 1, 4 * LANES)],
-        (u_array, parts, energy),
-        scalars=1,
-        name="holder_sum",
-    )
-    slices = exchange(slices, "view")
-    vertex_grad, rows = call(
-        project_kernel,
-        [(3, VIEWS * LANES), (HOLDERS, 1, 2 * LANES)],
-        (slices, shape_basis),
-        name="project",
-    )
-    total = exchange(rows, "vertex").sum(axis=(0, 1))
-    coeff_grad = total[: coeffs.shape[0]]
-    energy = jnp.sum(total[LANES:])
-    return (energy / pixels, vertex_grad, coeff_grad)
+        block_ids,
+        entries,
+        table,
+        pix_slot,
+        jnp.transpose(barycentric, (1, 0, 2)),
+        camera,
+        jnp.transpose(target, (1, 0, 2)),
+    )
+    returned = along_window(exchange(parts, "view").sum(axis=0), 1)
+    total = to_all(jnp.concatenate([returned, energy], axis=0), "view").sum(axis=0)
+    vertex_grad = total[:24].reshape(3, VIEWS * LANES)
+    coeff_part = jnp.sum(basis.astype(F32) * vertex_grad[:, None, :], axis=(0, 2))
+    energy_part = total[24:].sum(axis=0)
+    energy_part = energy_part[:shapes] + energy_part[shapes:]
+    rows = jnp.concatenate([coeff_part, energy_part]).reshape(1, 2 * shapes)
+    total = to_all(rows, "vertex").sum(axis=(0, 1))
+    return (jnp.sum(total[shapes:]) / pixels, vertex_grad, total[:shapes])
 
 
 def solution(mesh):

time: 136 us -> 107 us (0.79)
  blocking collectives: 53 us -> 39.9 us
  Pallas kernels: 20.5 us -> 10.2 us
  local copies, waits for them, and re-layouts: 10.5 us -> 5.55 us
  starting transfers between devices: 28.8 us -> 25.6 us
  other arithmetic: 2.58 us -> 4.05 us
    all_to_all x4 -> x3, blocking collectives: 53 us -> 39.9 us  [exchange(): return lax.all_to_all(array, axis, 0, 0, tiled=True)]
    all_to_all x3 -> x2, starting transfers between devices: 28.8 us -> 16.4 us  [exchange(): return lax.all_to_all(array, axis, 0, 0, tiled=True)]
    pallas_call x7 -> x1, Pallas kernels: 20.5 us -> 10.2 us  [call(): pl.pallas_call(kernel, out_shape=shapes[0] if single else shapes, in_spec...]
    ppermute x0 -> x2, waiting for transfers between devices: none -> 9.43 us  [along_window(): return lax.ppermute(array, ('vertex', 'view'), pairs)]
    ppermute x0 -> x2, starting transfers between devices: none -> 9.22 us  [along_window(): return lax.ppermute(array, ('vertex', 'view'), pairs)]
    all_to_all x3 -> x2, waiting for transfers between devices: 17.5 us -> 8.93 us  [exchange(): return lax.all_to_all(array, axis, 0, 0, tiled=True)]
    unnamed x29 -> x24, local copies, waits for them, and re-layouts: 7.99 us -> 3.27 us
    broadcast_in_dim x0 -> x5, local copies, waits for them, and re-layouts: none -> 1.4 us  [to_all(): return exchange(jnp.broadcast_to(array[None], (size, *array.shape)), axis)]
  transfers between devices with their start and end apart: 3 -> 4, of which waited for: 3 -> 4; matrix products, arithmetic and copies ran while one was open for 4% -> 2% of each run, Pallas kernels for 0% -> 0%
where the time goes in v2:
time: 107 us; the launch traced here: 106 us
  blocking collectives  39.9 us (37%)
  starting transfers between devices  25.6 us (24%)
  waiting for transfers between devices  18.4 us (17%)
  Pallas kernels  10.2 us (10%)
  local copies, waits for them, and re-layouts  5.55 us (5%)
  other arithmetic  4.05 us (4%)
  between operations  2.53 us (2%)
    all_to_all x3, blocking collectives, exchange(): return lax.all_to_all(array, axis, 0, 0, tiled=True)  39.9 us
    all_to_all x2, starting transfers between devices, exchange(): return lax.all_to_all(array, axis, 0, 0, tiled=True)  16.4 us
    pallas_call x1, Pallas kernels, call(): pl.pallas_call(kernel, out_shape=shapes[0] if single else shapes, in_spec...  10.2 us
    ppermute x2, waiting for transfers between devices, along_window(): return lax.ppermute(array, ('vertex', 'view'), pairs)  9.43 us
    ppermute x2, starting transfers between devices, along_window(): return lax.ppermute(array, ('vertex', 'view'), pairs)  9.22 us
    all_to_all x2, waiting for transfers between devices, exchange(): return lax.all_to_all(array, axis, 0, 0, tiled=True)  8.93 us
    unnamed x24, local copies, waits for them, and re-layouts  3.27 us
  transfers between devices with their start and end apart: 4, of which 4 were waited for; matrix products, arithmetic and copies ran while one was open for 2% of the time, Pallas kernels for 0%

profile of v2, /device:TPU:1, one launch (start us, length us, event | category | flops | bytes accessed | tf_op | source)
XLA Modules:
  0.0 106.2 jit_solution(1732754250962863401)
XLA Ops:
  0.6 0.7 convert_element_type.15
  1.3 1.2 %fusion = f32[3,1024]{1,0:T(4,128)S(1)} fusion(bf16[64,3,1024]{2,0,1:T(8,128)(2,1)} %param.11, f32[64]{0:T(128)S(1)} %convert_element_type.15), kind=kLoop, calls=%fused_computation.2 | loop fusion | flops 586752 | bytes 405760 | tf_op jit(solution)/shard_map/reduce_sum | solution.py:285
  2.5 0.6 broadcast_in_dim.11
  3.1 10.2 %all-to-all-start = ((f32[8,24,128]{2,1,0:T(8,128)}), f32[8,24,128]{2,1,0:T(8,128)S(1)}, u32[]{:S(2)}, u32[]{:S(2)}) async-start(f32[8,24,128]{2,1,0:T(8,128)} %broadcast_in_dim.11), calls=%async_computation | async-start | bytes 196608 | tf_op jit(solution)/shard_map/all_to_all | solution.py:207
  13.3 0.1 pad_add_fusion
  13.4 0.7 copy-done.4
  14.1 0.1 constant_dynamic-slice_fusion.1
  14.2 4.1 %all-to-all-done = f32[8,24,128]{2,1,0:T(8,128)S(1)} async-done(((f32[8,24,128]{2,1,0:T(8,128)}), f32[8,24,128]{2,1,0:T(8,128)S(1)}, u32[]{:S(2)}, u32[]{:S(2)}) %all-to-all-start) | async-done | bytes 98336 | tf_op jit(solution)/shard_map/all_to_all | solution.py:207
  18.4 1.9 %collective-permute-start = (f32[72,128]{1,0:T(8,128)S(1)}, f32[72,128]{1,0:T(8,128)S(1)}, u32[]{:S(2)}, u32[]{:S(2)}) collective-permute-start(f32[72,128]{1,0:T(8,128)S(1)} %pad_maximum_fusion), channel_id=1, source_target_pairs={{0,24},{1,17},{2,10},{3,3},{4,508},{5,501},{6,494},{7,263},{8,32},... | collective-permute-start | bytes 110600 | tf_op jit(solution)/shard_map/ppermute | solution.py:261
  20.3 0.1 constant_dynamic-slice_fusion
  20.4 0.1 copy.44
  20.5 0.1 copy.45
  20.6 0.5 copy-done.7
  21.1 0.1 copy.39
  21.1 8.6 %collective-permute-done = f32[72,128]{1,0:T(8,128)S(1)} collective-permute-done((f32[72,128]{1,0:T(8,128)S(1)}, f32[72,128]{1,0:T(8,128)S(1)}, u32[]{:S(2)}, u32[]{:S(2)}) %collective-permute-start) | collective-permute-done | bytes 36896 | tf_op jit(solution)/shard_map/ppermute | solution.py:261
  29.8 0.7 broadcast_in_dim.12
  30.5 6.2 %all-to-all-start.1 = ((f32[8,72,128]{2,1,0:T(8,128)}), f32[8,72,128]{2,1,0:T(8,128)S(1)}, u32[]{:S(2)}, u32[]{:S(2)}) async-start(f32[8,72,128]{2,1,0:T(8,128)} %broadcast_in_dim.12), calls=%async_computation.1 | async-start | bytes 589824 | tf_op jit(solution)/shard_map/all_to_all | solution.py:207
  36.7 0.7 reshape.23.entry_row_ref
  37.4 0.7 copy.42.camera_ref
  38.1 0.6 add_maximum_fusion.block_ref
  38.7 4.8 %all-to-all-done.1.table_ref = f32[8,72,128]{2,1,0:T(8,128)S(1)} async-done(((f32[8,72,128]{2,1,0:T(8,128)}), f32[8,72,128]{2,1,0:T(8,128)S(1)}, u32[]{:S(2)}, u32[]{:S(2)}) %all-to-all-start.1) | async-done | bytes 294944 | tf_op jit(solution)/shard_map/all_to_all | solution.py:207
  43.5 0.7 copy-done.1
  44.2 10.2 %tiles.1 = (f32[8,24,128]{2,1,0:T(8,128)}, f32[8,128]{1,0:T(8,128)}) custom-call(s32[8,4]{1,0:T(8,128)} %add_maximum_fusion.block_ref, s32[32,8]{1,0:T(8,128)} %copy-done.2, s32[1,256]{1,0:T(1,128)} %reshape.23.entry_row_ref, f32[8,72,128]{2,1,0:T(8,128)} %copy-done.1, s32[32,256]{1,0:T(8,128)} %slot_ref.1, f32[3,32,256]{2,1,0:T(8,128)} %bitcast.5, ...), custom_call_target="tpu_custom_call" | custom-call | tf_op jit(solution)/shard_map/tiles/pallas_call | solution.py:196
  54.3 9.5 %all_to_all.25 = f32[8,24,128]{2,1,0:T(8,128)S(1)} all-to-all(f32[8,24,128]{2,1,0:T(8,128)} %get-tuple-element.5), channel_id=1, replica_groups=mesh['vertex'=64,'view'=8] {'view'}, dimensions={0} | all-to-all | bytes 196608 | tf_op jit(solution)/shard_map/all_to_all | solution.py:207
  63.8 7.3 %collective-permute-start.1 = (f32[24,128]{1,0:T(8,128)S(1)}, f32[24,128]{1,0:T(8,128)S(1)}, u32[]{:S(2)}, u32[]{:S(2)}) collective-permute-start(f32[24,128]{1,0:T(8,128)S(1)} %reduce_sum.74), channel_id=1, source_target_pairs={{0,488},{1,497},{2,506},{3,3},{4,12},{5,21},{6,30},{7,263},{8,496}... | collective-permute-start | bytes 36872 | tf_op jit(solution)/shard_map/ppermute | solution.py:261
  71.1 0.8 collective-permute-done.1
  72.0 11.0 %all_to_all.26 = f32[8,32,128]{2,1,0:T(8,128)S(1)} all-to-all(f32[8,32,128]{2,1,0:T(8,128)S(1)} %broadcast_in_dim.13), channel_id=1, replica_groups=mesh['vertex'=64,'view'=8] {'view'}, dimensions={0} | all-to-all | bytes 262144 | tf_op jit(solution)/shard_map/all_to_all | solution.py:207
  83.0 0.2 fusion.1
  83.2 0.4 copy-done.3
  83.7 0.1 pad_maximum_fusion.2
  83.8 19.5 %all_to_all.27 = f32[64,1,128]{2,1,0:T(1,128)S(1)} all-to-all(f32[64,1,128]{2,1,0:T(1,128)S(1)} %broadcast_in_dim.14), channel_id=1, replica_groups=mesh['vertex'=64,'view'=8] {'vertex'}, dimensions={0} | all-to-all | bytes 65536 | tf_op jit(solution)/shard_map/all_to_all | solution.py:207
  103.3 1.1 %fusion.2 = (f32[64]{0:T(128)}, f32[]{:T(128)}) fusion(f32[128]{0:T(128)S(1)} %reduce_sum.78), kind=kLoop, calls=%fused_computation.15 | loop fusion | flops 63 | bytes 772 | tf_op jit(solution)/shard_map/slice | solution.py:307
  (34 shorter events, 0.3 us)
Async XLA Ops:
  3.1 10.2 %copy-start.9 = (s32[1,64,4]{1,2,0:T(4,128)S(1)}, s32[1,64,4]{1,2,0:T(4,128)}, u32[]{:S(2)}) copy-start(s32[1,64,4]{1,2,0:T(4,128)} %param.14) | copy-start | bytes 3076
  3.1 10.3 %copy-start.5 = (f32[3,1024]{1,0:T(4,128)S(1)}, f32[3,1024]{1,0:T(4,128)}, u32[]{:S(2)}) copy-start(f32[3,1024]{1,0:T(4,128)} %param.12) | copy-start | bytes 36868
  3.1 15.2 %all-to-all-start = ((f32[8,24,128]{2,1,0:T(8,128)}), f32[8,24,128]{2,1,0:T(8,128)S(1)}, u32[]{:S(2)}, u32[]{:S(2)}) async-start(f32[8,24,128]{2,1,0:T(8,128)} %broadcast_in_dim.11), calls=%async_computation | async-start | bytes 196608 | tf_op jit(solution)/shard_map/all_to_all | solution.py:207
  13.3 0.8 copy-start.4
  18.4 11.4 %collective-permute-start = (f32[72,128]{1,0:T(8,128)S(1)}, f32[72,128]{1,0:T(8,128)S(1)}, u32[]{:S(2)}, u32[]{:S(2)}) collective-permute-start(f32[72,128]{1,0:T(8,128)S(1)} %pad_maximum_fusion), channel_id=1, source_target_pairs={{0,24},{1,17},{2,10},{3,3},{4,508},{5,501},{6,494},{7,263},{8,32},... | collective-permute-start | bytes 110600 | tf_op jit(solution)/shard_map/ppermute | solution.py:261
  20.4 0.7 copy-start.7
  30.5 13.0 %all-to-all-start.1 = ((f32[8,72,128]{2,1,0:T(8,128)}), f32[8,72,128]{2,1,0:T(8,128)S(1)}, u32[]{:S(2)}, u32[]{:S(2)}) async-start(f32[8,72,128]{2,1,0:T(8,128)} %broadcast_in_dim.12), calls=%async_computation.1 | async-start | bytes 589824 | tf_op jit(solution)/shard_map/all_to_all | solution.py:207
  36.7 1.4 %copy-start.2 = (s32[32,8]{1,0:T(8,128)}, s32[32,8]{1,0:T(8,128)S(1)}, u32[]{:S(2)}) copy-start(s32[32,8]{1,0:T(8,128)S(1)} %and_add_fusion.entry_ref) | copy-start | bytes 3076
  36.7 0.7 copy-start.6
  43.5 0.7 copy-start.1
  54.3 17.6 %copy-start.8 = (f32[8,128]{1,0:T(8,128)S(1)}, f32[8,128]{1,0:T(8,128)}, u32[]{:S(2)}) copy-start(f32[8,128]{1,0:T(8,128)} %get-tuple-element.6) | copy-start | bytes 12292
  63.8 19.2 %copy-start = (bf16[64,3,1024]{2,0,1:T(8,128)(2,1)S(1)}, bf16[64,3,1024]{2,0,1:T(8,128)(2,1)}, u32[]{:S(2)}) copy-start(bf16[64,3,1024]{2,0,1:T(8,128)(2,1)} %param.11) | copy-start | bytes 1179652
  63.8 8.1 %collective-permute-start.1 = (f32[24,128]{1,0:T(8,128)S(1)}, f32[24,128]{1,0:T(8,128)S(1)}, u32[]{:S(2)}, u32[]{:S(2)}) collective-permute-start(f32[24,128]{1,0:T(8,128)S(1)} %reduce_sum.74), channel_id=1, source_target_pairs={{0,488},{1,497},{2,506},{3,3},{4,12},{5,21},{6,30},{7,263},{8,496}... | collective-permute-start | bytes 36872 | tf_op jit(solution)/shard_map/ppermute | solution.py:261
  83.0 0.6 copy-start.3

commit v3 on v2

v3 whole, which is shorter than its diff:
```python
import jax
import jax.numpy as jnp
from jax import lax
from jax.experimental import pallas as pl
from jax.experimental.pallas import tpu as pltpu
from jax.sharding import PartitionSpec as P

LANES = 128
SMOOTH = 0.1
VIEWS = 8
HOLDERS = 64
UNROLL_GATHER = 32
UNROLL_SCATTER = 32
OFFSETS = (-3, -2, -1, 0, 1, 2, 3, 32)
WIN = len(OFFSETS)
CAP = 4
COVER = 8
TILES = 32
BLOCKS = 16
SHARD = 24 + 3 * BLOCKS

F32 = jnp.float32
BF16 = jnp.bfloat16
VMEM = pl.BlockSpec(memory_space=pltpu.VMEM)
SMEM = pl.BlockSpec(memory_space=pltpu.SMEM)


def pick_lanes(source, lane):
    return jnp.take_along_axis(source, lane, axis=1, mode="promise_in_bounds")


def high_low(values):
    high = values.astype(BF16).astype(F32)
    return jnp.concatenate([high, values - high], axis=0).astype(BF16)


def lane_onehot(lane_row, ids):
    row = jnp.broadcast_to(lane_row.astype(F32), (16, LANES)).astype(BF16)
    one = jnp.ones((16, LANES), BF16)
    zero = jnp.zeros((16, LANES), BF16)
    return jnp.concatenate([jnp.where(i == row, one, zero) for i in ids], axis=0)


def dot_nt(a, b):
    return lax.dot_general(a, b, (((1,), (1,)), ((), ())), preferred_element_type=F32)


def entry_of(cover, u):
    relative = ((cover >> 2) - u + 3) & (HOLDERS - 1)
    return jnp.minimum(relative, WIN - 1) * CAP + (cover & (CAP - 1))


def tile_kernel(
    u_ref,
    fetch_ref,
    cover_ref,
    cover_rows_ref,
    table_ref,
    slot_ref,
    weight_ref,
    camera_ref,
    target_ref,
    out_ref,
    energy_ref,
    slot_rows,
    corner_id,
    entry_table,
    last_table,
    tile_last,
    corner_pix,
    grad_pix,
    tile_grad,
    entry_grad,
):
    u = u_ref[0]
    sub8 = lax.broadcasted_iota(jnp.int32, (8, LANES), 0)
    sub16 = lax.broadcasted_iota(jnp.int32, (16, LANES), 0)
    ids16 = [(sub16 + 16 * i).astype(F32).astype(BF16) for i in range(8)]
    for half in range(2):
        slot_rows[half * TILES : (half + 1) * TILES, :] = slot_ref[
            :, half * LANES : (half + 1) * LANES
        ]
    for j in range(WIN):
        for s in range(CAP):
            block = jnp.maximum(fetch_ref[s, (u + OFFSETS[j]) & (HOLDERS - 1)], 0)
            for c in range(3):
                ids = table_ref[j, pl.ds(24 + c * BLOCKS + block, 1), :]
                corner_id[pl.ds(j * 16 + c * CAP + s, 1), :] = ids.astype(jnp.int32)
    for j in range(WIN):
        ids = [corner_id[pl.ds(j * 16 + 8 * i, 8), :] for i in range(2)]
        lane = [i & (LANES - 1) for i in ids]
        sub = [i >> 7 for i in ids]
        for d in range(3):
            found = [jnp.zeros((8, LANES), F32)] * 2
            for s in range(8):
                source = jnp.broadcast_to(
                    table_ref[j, 8 * d + s : 8 * d + s + 1, :], (8, LANES)
                )
                for i in range(2):
                    found[i] = jnp.where(sub[i] == s, pick_lanes(source, lane[i]), found[i])
            for c in range(3):
                rows = found[c // 2][(c % 2) * CAP : (c % 2) * CAP + CAP]
                if 3 * c + d < 8:
                    entry_table[pl.ds(j * 32 + 3 * c + d, CAP, stride=8), :] = rows
                else:
                    last_table[pl.ds(j * CAP, CAP), :] = rows

    def gather_tile(t, carry):
        entries = [entry_of(cover_ref[n, t], u) for n in range(COVER)]
        base = pl.multiple_of(t * 8, 8)
        for n in range(COVER):
            tile_last[pl.ds(base + n, 1), :] = last_table[pl.ds(entries[n], 1), :]
        last = tile_last[pl.ds(base, 8), :]
        for half in range(2):
            q = slot_rows[pl.ds(half * TILES + t, 1), :]
            q = jnp.broadcast_to(q, (8, LANES))
            lane = q & (LANES - 1)
            which = q >> 7
            first = jnp.zeros((8, LANES), F32)
            for n in range(COVER):
                at = pl.multiple_of(entries[n] * 8, 8)
                picked = pick_lanes(entry_table[pl.ds(at, 8), :], lane)
                first = jnp.where(which == n, picked, first)
            second = jnp.where(which == sub8, pick_lanes(last, lane), 0.0)
            row = half * TILES + t
            corner_pix[pl.ds(row, 8, stride=2 * TILES), :] = first
            corner_pix[pl.ds(8 * 2 * TILES + row, 1), :] = jnp.sum(
                second, axis=0, keepdims=True
            )
        return carry

    lax.fori_loop(0, TILES, gather_tile, 0, unroll=UNROLL_GATHER)

    camera = camera_ref[...].T
    energy = jnp.zeros((TILES, LANES), F32)
    for half in range(2):
        cols = slice(half * LANES, (half + 1) * LANES)
        weights = [weight_ref[c, :, cols] for c in range(3)]

        def rows_of(cd):
            return pl.ds(cd * 2 * TILES + half * TILES, TILES)

        surface = []
        for d in range(3):
            value = weights[0] * corner_pix[rows_of(d), :]
            value = value + weights[1] * corner_pix[rows_of(3 + d), :]
            surface.append(value + weights[2] * corner_pix[rows_of(6 + d), :])
        grad_surface = [jnp.zeros((TILES, LANES), F32)] * 3
        for r in range(3):
            matrix = [camera[:, 3 * r + d : 3 * r + d + 1] for d in range(3)]
            linear = matrix[0] * surface[0]
            linear = linear + matrix[1] * surface[1]
            linear = linear + matrix[2] * surface[2]
            shaded = jnp.tanh(linear + camera[:, 9 + r : 10 + r])
            differ = shaded - target_ref[r, :, cols]
            square = differ * differ + SMOOTH * SMOOTH
            inverse = lax.rsqrt(square)
            energy = energy + square * inverse
            grad_linear = differ * inverse * (1.0 - shaded * shaded)
            for d in range(3):
                grad_surface[d] = grad_surface[d] + matrix[d] * grad_linear
        for c in range(3):
            for d in range(3):
                grad = weights[c] * grad_surface[d]
                high = grad.astype(BF16).astype(F32)
                grad_pix[rows_of(3 * c + d), :] = high
                grad_pix[rows_of(9 + 3 * c + d), :] = grad - high
    energy_ref[...] = energy[0:8] + energy[8:16] + energy[16:24] + energy[24:32]

    def scatter_tile(t, carry):
        spread_rows = [[] for _ in range(18)]
        onehot = []
        for half in range(2):
            q = slot_rows[pl.ds(half * TILES + t, 1), :]
            mine = jnp.broadcast_to(q >> 7, (8, LANES)) == sub8
            onehot.append(lane_onehot(q & (LANES - 1), ids16))
            for cd in range(18):
                grad = grad_pix[pl.ds(cd * 2 * TILES + half * TILES + t, 1), :]
                grad = jnp.broadcast_to(grad, (8, LANES))
                spread_rows[cd].append(jnp.where(mine, grad, 0.0))
        rows = jnp.concatenate([jnp.concatenate(r, axis=1) for r in spread_rows], axis=0)
        summed = dot_nt(rows.astype(BF16), jnp.concatenate(onehot, axis=1))
        summed = summed[:72] + summed[72:]
        for cd in range(9):
            tile_grad[pl.ds(cd * COVER * TILES + t, COVER, stride=TILES), :] = summed[
                8 * cd : 8 * cd + 8
            ]
        return carry

    lax.fori_loop(0, TILES, scatter_tile, 0, unroll=UNROLL_SCATTER)

    entry_rows = entry_of(cover_rows_ref[...], u)
    entry_rows = jnp.concatenate([entry_rows[n : n + 1] for n in range(COVER)], axis=1)
    entry_ids = lax.broadcasted_iota(jnp.int32, (WIN * CAP, TILES * COVER), 0)
    pick = jnp.where(entry_ids == entry_rows, 1.0, 0.0).astype(BF16)
    for cd in range(9):
        values = tile_grad[pl.ds(cd * COVER * TILES, COVER * TILES), :]
        high = values.astype(BF16)
        low = (values - high.astype(F32)).astype(BF16)
        both = jnp.dot(
            pick, jnp.concatenate([high, low], axis=1), preferred_element_type=F32
        )
        entry_grad[pl.ds(cd * WIN * CAP, WIN * CAP), :] = both[:, :LANES] + both[:, LANES:]

    for j in range(WIN):
        rows = [[] for _ in range(3)]
        onehot = []
        for c in range(3):
            for s in range(CAP):
                ids = corner_id[pl.ds(j * 16 + c * CAP + s, 1), :]
                mine = jnp.broadcast_to(ids >> 7, (8, LANES)) == sub8
                onehot.append(lane_onehot(ids & (LANES - 1), ids16))
                for d in range(3):
                    at = (3 * c + d) * WIN * CAP + j * CAP + s
                    grad = jnp.broadcast_to(entry_grad[pl.ds(at, 1), :], (8, LANES))
                    rows[d].append(jnp.where(mine, grad, 0.0))
        stacked = jnp.concatenate([jnp.concatenate(r, axis=1) for r in rows], axis=0)
        summed = dot_nt(high_low(stacked), jnp.concatenate(onehot, axis=1))
        out_ref[j] = summed[:24] + summed[24:]


def call(kernel, out_shapes, args, scalars=0, scratch=(), name=None):
    shapes = [jax.ShapeDtypeStruct(s, F32) for s in out_shapes]
    single = len(shapes) == 1
    return pl.pallas_call(
        kernel,
        out_shape=shapes[0] if single else shapes,
        in_specs=[SMEM] * scalars + [VMEM] * (len(args) - scalars),
        out_specs=VMEM if single else [VMEM] * len(shapes),
        scratch_shapes=list(scratch),
        name=name,
    )(*args)


def exchange(array, axis):
    return lax.all_to_all(array, axis, 0, 0, tiled=True)


def tile_call(u, fetch_list, tile_cover, table, pix_slot, barycentric, camera, target):
    return call(
        tile_kernel,
        [(WIN, 24, LANES), (8, LANES)],
        (
            u.reshape(1),
            fetch_list,
            tile_cover,
            tile_cover,
            table,
            pix_slot,
            barycentric,
            camera,
            target,
        ),
        scalars=3,
        scratch=(
            pltpu.VMEM((2 * TILES, LANES), jnp.int32),
            pltpu.VMEM((16 * WIN, LANES), jnp.int32),
            pltpu.VMEM((8 * WIN * CAP, LANES), F32),
            pltpu.VMEM((WIN * CAP, LANES), F32),
            pltpu.VMEM((8 * TILES, LANES), F32),
            pltpu.VMEM((9 * 2 * TILES, LANES), F32),
            pltpu.VMEM((18 * 2 * TILES, LANES), F32),
            pltpu.VMEM((9 * TILES * COVER, LANES), F32),
            pltpu.VMEM((9 * WIN * CAP, LANES), F32),
        ),
        name="tiles",
    )


def to_all(array, axis):
    size = lax.axis_size(axis)
    return exchange(jnp.broadcast_to(array[None], (size, *array.shape)), axis)


def along_window(array, sign):
    holders = lax.axis_size("vertex")
    pairs = [
        (h * VIEWS + j, (h + sign * OFFSETS[j]) % holders * VIEWS + j)
        for h in range(holders)
        for j in range(VIEWS)
    ]
    return lax.ppermute(array, ("vertex", "view"), pairs)


def per_device(
    coeffs,
    shape_basis,
    rest_pose,
    triangles,
    fetch_list,
    tile_cover,
    pix_slot,
    barycentric,
    camera,
    target,
):
    u = lax.axis_index("vertex").astype(jnp.int32)
    pixels = (
        tile_cover.shape[0] * pix_slot.shape[1] * lax.axis_size("vertex") * lax.axis_size("view")
    )
    shapes = coeffs.shape[0]
    basis = jnp.transpose(shape_basis, (1, 0, 2))
    partial = lax.dot_general(
        coeffs[None], basis, (((1,), (1,)), ((), ())), preferred_element_type=F32
    )
    rest = rest_pose.reshape(24, LANES)
    corners = triangles.reshape(3 * BLOCKS, LANES).astype(F32)
    u, partial, rest, corners = lax.optimization_barrier((u, partial, rest, corners))
    positions = rest + to_all(partial.reshape(24, LANES), "view").sum(axis=0)
    shard = along_window(jnp.concatenate([positions, corners], axis=0), -1)
    table = to_all(shard, "view")
    parts, energy = tile_call(
        u,
        jnp.transpose(fetch_list[0]),
        jnp.transpose(tile_cover),
        table,
        pix_slot,
        jnp.transpose(barycentric, (1, 0, 2)),
        jnp.transpose(camera),
        jnp.transpose(target, (1, 0, 2)),
    )
    returned = along_window(exchange(parts, "view").sum(axis=0), 1)
    total = to_all(jnp.concatenate([returned, energy], axis=0), "view").sum(axis=0)
    vertex_grad = total[:24].reshape(3, VIEWS * LANES)
    coeff_part = jnp.sum(basis.astype(F32) * vertex_grad[:, None, :], axis=(0, 2))
    energy_part = total[24:].sum(axis=0)
    energy_part = energy_part[:shapes] + energy_part[shapes:]
    rows = jnp.concatenate([coeff_part, energy_part]).reshape(1, 2 * shapes)
    total = to_all(rows, "vertex").sum(axis=(0, 1))
    return (jnp.sum(total[shapes:]) / pixels, vertex_grad, total[:shapes])


def solution(mesh):
    placed = (
        P("view"),
        P("view", None, "vertex"),
        P(None, "vertex"),
        P(None, "vertex"),
        P(("vertex", "view"), None, None),
        P(("vertex", "view"), None),
        P(("vertex", "view"), None),
        P(("vertex", "view"), None, None),
        P(("vertex", "view"), None),
        P(("vertex", "view"), None, None),
    )
    return jax.shard_map(
        per_device,
        mesh=mesh,
        in_specs=placed,
        out_specs=(P(), P(None, "vertex"), P("view")),
        check_vma=False,
    )
```

time: 107 us -> 102 us (0.953)
  blocking collectives: 39.9 us -> 66.8 us
  starting transfers between devices: 25.6 us -> 9.41 us
  waiting for transfers between devices: 18.4 us -> 11 us
  local copies, waits for them, and re-layouts: 5.55 us -> 1.92 us
  Pallas kernels: 10.2 us -> 6.96 us
  other arithmetic: 4.05 us -> 1.54 us
  matrix products: 0 us -> 1.17 us
    all_to_all x3 -> x5, blocking collectives: 39.9 us -> 66.8 us  [exchange(): return lax.all_to_all(array, axis, 0, 0, tiled=True)]
    all_to_all x2 -> x0, starting transfers between devices: 16.4 us -> none  [exchange(): return lax.all_to_all(array, axis, 0, 0, tiled=True)]
    all_to_all x2 -> x0, waiting for transfers between devices: 8.93 us -> none  [exchange(): return lax.all_to_all(array, axis, 0, 0, tiled=True)]
    pallas_call x1, Pallas kernels: 10.2 us -> 6.96 us  [call(): pl.pallas_call(kernel, out_shape=shapes[0] if single else shapes, in_spec...]
    ppermute x2, waiting for transfers between devices: 9.43 us -> 11 us  [along_window(): return lax.ppermute(array, ('vertex', 'view'), pairs)]
    unnamed x24 -> x12, local copies, waits for them, and re-layouts: 3.27 us -> 1.8 us
    broadcast_in_dim x5, local copies, waits for them, and re-layouts: 1.4 us -> 0.07 us  [to_all(): return exchange(jnp.broadcast_to(array[None], (size, *array.shape)), axis)]
    dot_general x0 -> x1, matrix products: none -> 1.17 us  [per_device(): lax.dot_general(coeffs[None], basis, (((1,), (1,)), ((), ())), preferred_...]
  transfers between devices with their start and end apart: 4 -> 2, of which waited for: 4 -> 2; matrix products, arithmetic and copies ran while one was open for 2% -> 0% of each run, Pallas kernels for 0% -> 0%
where the time goes in v3:
time: 102 us; the launch traced here: 101 us
  blocking collectives  66.8 us (65%)
  waiting for transfers between devices  11 us (11%)
  starting transfers between devices  9.41 us (9%)
  Pallas kernels  6.96 us (7%)
  between operations  2.53 us (2%)
  local copies, waits for them, and re-layouts  1.92 us (2%)
  other arithmetic  1.54 us (2%)
  matrix products  1.17 us (1%)
    all_to_all x5, blocking collectives, exchange(): return lax.all_to_all(array, axis, 0, 0, tiled=True)  66.8 us
    ppermute x2, waiting for transfers between devices, along_window(): return lax.ppermute(array, ('vertex', 'view'), pairs)  11 us
    ppermute x2, starting transfers between devices, along_window(): return lax.ppermute(array, ('vertex', 'view'), pairs)  9.41 us
    pallas_call x1, Pallas kernels, call(): pl.pallas_call(kernel, out_shape=shapes[0] if single else shapes, in_spec...  6.96 us
  transfers between devices with their start and end apart: 2, of which 2 were waited for; matrix products, arithmetic and copies ran while one was open for 0% of the time, Pallas kernels for 0%

profile of v3, /device:TPU:1, one launch (start us, length us, event | category | flops | bytes accessed | tf_op | source)
XLA Modules:
  0.0 101.3 jit_solution(11101271295616050792)
XLA Ops:
  0.6 0.0 copy-start
  0.6 0.6 copy-done
  1.3 0.0 copy-start.4
  1.3 1.2 %fusion = f32[1,3,1024]{2,0,1:T(1,128)S(1)} fusion(bf16[64,3,1024]{2,0,1:T(8,128)(2,1)} %param.11, bf16[64]{0:T(256)(128)(2,1)S(1)} %copy-done), kind=kOutput, calls=%fused_computation.1 | convolution fusion | flops 393216 | bytes 405632 | tf_op jit(solution)/shard_map/dot_general | solution.py:303
  2.5 0.0 copy-start.3
  2.5 0.0 copy-done.4
  2.5 0.7 copy-done.3
  3.3 14.2 %all_to_all.25 = f32[8,24,128]{2,1,0:T(8,128)S(1)} all-to-all(f32[8,24,128]{2,1,0:T(8,128)S(1)} %broadcast_in_dim.11), channel_id=1, replica_groups=mesh['vertex'=64,'view'=8] {'view'}, dimensions={0} | all-to-all | bytes 196608 | tf_op jit(solution)/shard_map/all_to_all | solution.py:236
  17.5 1.9 %collective-permute-start = (f32[72,128]{1,0:T(8,128)S(1)}, f32[72,128]{1,0:T(8,128)S(1)}, u32[]{:S(2)}, u32[]{:S(2)}) collective-permute-start(f32[72,128]{1,0:T(8,128)S(1)} %pad_maximum_fusion), channel_id=1, source_target_pairs={{0,24},{1,17},{2,10},{3,3},{4,508},{5,501},{6,494},{7,263},{8,32},... | collective-permute-start | bytes 110600 | tf_op jit(solution)/shard_map/ppermute | solution.py:282
  19.5 10.2 %collective-permute-done = f32[72,128]{1,0:T(8,128)S(1)} collective-permute-done((f32[72,128]{1,0:T(8,128)S(1)}, f32[72,128]{1,0:T(8,128)S(1)}, u32[]{:S(2)}, u32[]{:S(2)}) %collective-permute-start) | collective-permute-done | bytes 36896 | tf_op jit(solution)/shard_map/ppermute | solution.py:282
  29.6 13.2 %all_to_all.26.table_ref = f32[8,72,128]{2,1,0:T(8,128)} all-to-all(f32[8,72,128]{2,1,0:T(8,128)S(1)} %broadcast_in_dim.12), channel_id=1, replica_groups=mesh['vertex'=64,'view'=8] {'view'}, dimensions={0} | all-to-all | bytes 589824 | tf_op jit(solution)/shard_map/all_to_all | solution.py:236
  42.9 7.0 %tiles.1 = (f32[8,24,128]{2,1,0:T(8,128)}, f32[8,128]{1,0:T(8,128)}) custom-call(s32[1]{0:T(128)} %bitcast.3.u_ref, s32[4,64]{1,0:T(4,128)} %bitcast.23, s32[8,32]{1,0:T(8,128)} %bitcast.20, s32[8,32]{1,0:T(8,128)} %bitcast.21, f32[8,72,128]{2,1,0:T(8,128)} %all_to_all.26.table_ref, s32[32,256]{1,0:T(8,128)} %slot_ref.1, f32[3,32,256]{2,1,0:T(8,128)} %bitcast.18, ...), custom_call_target="tpu_custom_call" | custom-call | tf_op jit(solution)/shard_map/tiles/pallas_call | solution.py:225
  49.8 0.0 copy-start.5
  49.8 8.9 %all_to_all.27 = f32[8,24,128]{2,1,0:T(8,128)S(1)} all-to-all(f32[8,24,128]{2,1,0:T(8,128)} %get-tuple-element.13), channel_id=1, replica_groups=mesh['vertex'=64,'view'=8] {'view'}, dimensions={0} | all-to-all | bytes 196608 | tf_op jit(solution)/shard_map/all_to_all | solution.py:236
  58.8 0.0 copy-start.1
  58.8 7.5 %collective-permute-start.1 = (f32[24,128]{1,0:T(8,128)S(1)}, f32[24,128]{1,0:T(8,128)S(1)}, u32[]{:S(2)}, u32[]{:S(2)}) collective-permute-start(f32[24,128]{1,0:T(8,128)S(1)} %reduce_sum.64), channel_id=1, source_target_pairs={{0,488},{1,497},{2,506},{3,3},{4,12},{5,21},{6,30},{7,263},{8,496}... | collective-permute-start | bytes 36872 | tf_op jit(solution)/shard_map/ppermute | solution.py:282
  66.3 0.8 collective-permute-done.1
  67.1 0.0 copy-done.5
  67.1 10.8 %all_to_all.28 = f32[8,32,128]{2,1,0:T(8,128)S(1)} all-to-all(f32[8,32,128]{2,1,0:T(8,128)S(1)} %broadcast_in_dim.13), channel_id=1, replica_groups=mesh['vertex'=64,'view'=8] {'view'}, dimensions={0} | all-to-all | bytes 262144 | tf_op jit(solution)/shard_map/all_to_all | solution.py:236
  78.0 0.1 slice_add_fusion
  78.1 0.0 copy-done.1
  78.1 0.0 copy-start.2
  78.1 0.2 multiply_reduce_fusion
  78.3 0.4 copy-done.2
  78.7 0.1 pad_maximum_fusion.2
  78.8 19.6 %all_to_all.29 = f32[64,1,128]{2,1,0:T(1,128)S(1)} all-to-all(f32[64,1,128]{2,1,0:T(1,128)S(1)} %broadcast_in_dim.14), channel_id=1, replica_groups=mesh['vertex'=64,'view'=8] {'vertex'}, dimensions={0} | all-to-all | bytes 65536 | tf_op jit(solution)/shard_map/all_to_all | solution.py:236
  98.4 1.1 %fusion.3 = (f32[64]{0:T(128)}, f32[]{:T(128)}) fusion(f32[128]{0:T(128)S(1)} %reduce_sum.68), kind=kLoop, calls=%fused_computation.10 | loop fusion | flops 63 | bytes 772 | tf_op jit(solution)/shard_map/slice | solution.py:330
  (19 shorter events, 0.2 us)
Async XLA Ops:
  0.6 0.7 copy-start
  1.3 1.2 %copy-start.4 = (f32[3,1024]{1,0:T(4,128)S(1)}, f32[3,1024]{1,0:T(4,128)}, u32[]{:S(2)}) copy-start(f32[3,1024]{1,0:T(4,128)} %param.12) | copy-start | bytes 36868
  2.5 0.8 copy-start.3
  17.5 12.1 %collective-permute-start = (f32[72,128]{1,0:T(8,128)S(1)}, f32[72,128]{1,0:T(8,128)S(1)}, u32[]{:S(2)}, u32[]{:S(2)}) collective-permute-start(f32[72,128]{1,0:T(8,128)S(1)} %pad_maximum_fusion), channel_id=1, source_target_pairs={{0,24},{1,17},{2,10},{3,3},{4,508},{5,501},{6,494},{7,263},{8,32},... | collective-permute-start | bytes 110600 | tf_op jit(solution)/shard_map/ppermute | solution.py:282
  49.8 17.3 %copy-start.5 = (f32[8,128]{1,0:T(8,128)S(1)}, f32[8,128]{1,0:T(8,128)}, u32[]{:S(2)}) copy-start(f32[8,128]{1,0:T(8,128)} %get-tuple-element.14) | copy-start | bytes 12292
  58.8 19.3 %copy-start.1 = (bf16[64,3,1024]{2,0,1:T(8,128)(2,1)S(1)}, bf16[64,3,1024]{2,0,1:T(8,128)(2,1)}, u32[]{:S(2)}) copy-start(bf16[64,3,1024]{2,0,1:T(8,128)(2,1)} %param.11) | copy-start | bytes 1179652
  58.8 8.3 %collective-permute-start.1 = (f32[24,128]{1,0:T(8,128)S(1)}, f32[24,128]{1,0:T(8,128)S(1)}, u32[]{:S(2)}, u32[]{:S(2)}) collective-permute-start(f32[24,128]{1,0:T(8,128)S(1)} %reduce_sum.64), channel_id=1, source_target_pairs={{0,488},{1,497},{2,506},{3,3},{4,12},{5,21},{6,30},{7,263},{8,496}... | collective-permute-start | bytes 36872 | tf_op jit(solution)/shard_map/ppermute | solution.py:282
  78.1 0.6 copy-start.2

commit v4 on v3

--- a/solution.py
+++ b/solution.py
@@ -52,9 +52,9 @@
 
 def tile_kernel(
     u_ref,
-    fetch_ref,
-    cover_ref,
+    fetch_rows_ref,
     cover_rows_ref,
+    cover_line_ref,
     table_ref,
     slot_ref,
     weight_ref,
@@ -62,17 +62,27 @@
     target_ref,
     out_ref,
     energy_ref,
+    fetch_ref,
+    entry_ref,
+    entry_rows,
+    sems,
     slot_rows,
     corner_id,
     entry_table,
     last_table,
     tile_last,
     corner_pix,
+    last_pix,
     grad_pix,
     tile_grad,
     entry_grad,
 ):
     u = u_ref[0]
+    fetch_copy = pltpu.make_async_copy(fetch_rows_ref, fetch_ref, sems.at[0])
+    fetch_copy.start()
+    entry_rows[...] = entry_of(cover_rows_ref[...], u) * 8
+    entry_copy = pltpu.make_async_copy(entry_rows, entry_ref, sems.at[1])
+    entry_copy.start()
     sub8 = lax.broadcasted_iota(jnp.int32, (8, LANES), 0)
     sub16 = lax.broadcasted_iota(jnp.int32, (16, LANES), 0)
     ids16 = [(sub16 + 16 * i).astype(F32).astype(BF16) for i in range(8)]
@@ -80,9 +90,10 @@
         slot_rows[half * TILES : (half + 1) * TILES, :] = slot_ref[
             :, half * LANES : (half + 1) * LANES
         ]
+    fetch_copy.wait()
     for j in range(WIN):
         for s in range(CAP):
-            block = jnp.maximum(fetch_ref[s, (u + OFFSETS[j]) & (HOLDERS - 1)], 0)
+            block = fetch_ref[s, (u + OFFSETS[j]) & (HOLDERS - 1)]
             for c in range(3):
                 ids = table_ref[j, pl.ds(24 + c * BLOCKS + block, 1), :]
                 corner_id[pl.ds(j * 16 + c * CAP + s, 1), :] = ids.astype(jnp.int32)
@@ -103,10 +114,12 @@
                 if 3 * c + d < 8:
                     entry_table[pl.ds(j * 32 + 3 * c + d, CAP, stride=8), :] = rows
                 else:
-                    last_table[pl.ds(j * CAP, CAP), :] = rows
+                    last_table[pl.ds(j * 32, CAP, stride=8), :] = rows
+
+    entry_copy.wait()
 
     def gather_tile(t, carry):
-        entries = [entry_of(cover_ref[n, t], u) for n in range(COVER)]
+        entries = [entry_ref[n, t] for n in range(COVER)]
         base = pl.multiple_of(t * 8, 8)
         for n in range(COVER):
             tile_last[pl.ds(base + n, 1), :] = last_table[pl.ds(entries[n], 1), :]
@@ -118,20 +131,18 @@
             which = q >> 7
             first = jnp.zeros((8, LANES), F32)
             for n in range(COVER):
-                at = pl.multiple_of(entries[n] * 8, 8)
+                at = pl.multiple_of(entries[n], 8)
                 picked = pick_lanes(entry_table[pl.ds(at, 8), :], lane)
                 first = jnp.where(which == n, picked, first)
             second = jnp.where(which == sub8, pick_lanes(last, lane), 0.0)
             row = half * TILES + t
-            corner_pix[pl.ds(row, 8, stride=2 * TILES), :] = first
-            corner_pix[pl.ds(8 * 2 * TILES + row, 1), :] = jnp.sum(
-                second, axis=0, keepdims=True
-            )
+            corner_pix[pl.ds(pl.multiple_of(row * 8, 8), 8), :] = first
+            last_pix[pl.ds(row, 1), :] = jnp.sum(second, axis=0, keepdims=True)
         return carry
 
     lax.fori_loop(0, TILES, gather_tile, 0, unroll=UNROLL_GATHER)
 
-    camera = camera_ref[...].T
+    camera = camera_ref[...]
     energy = jnp.zeros((TILES, LANES), F32)
     for half in range(2):
         cols = slice(half * LANES, (half + 1) * LANES)
@@ -140,11 +151,15 @@
         def rows_of(cd):
             return pl.ds(cd * 2 * TILES + half * TILES, TILES)
 
+        def corner(cd):
+            if cd == 8:
+                return last_pix[half * TILES : (half + 1) * TILES, :]
+            return corner_pix[pl.ds(half * TILES * 8 + cd, TILES, stride=8), :]
+
         surface = []
         for d in range(3):
-            value = weights[0] * corner_pix[rows_of(d), :]
-            value = value + weights[1] * corner_pix[rows_of(3 + d), :]
-            surface.append(value + weights[2] * corner_pix[rows_of(6 + d), :])
+            value = weights[0] * corner(d) + weights[1] * corner(3 + d)
+            surface.append(value + weights[2] * corner(6 + d))
         grad_surface = [jnp.zeros((TILES, LANES), F32)] * 3
         for r in range(3):
             matrix = [camera[:, 3 * r + d : 3 * r + d + 1] for d in range(3)]
@@ -182,17 +197,15 @@
         summed = dot_nt(rows.astype(BF16), jnp.concatenate(onehot, axis=1))
         summed = summed[:72] + summed[72:]
         for cd in range(9):
-            tile_grad[pl.ds(cd * COVER * TILES + t, COVER, stride=TILES), :] = summed[
-                8 * cd : 8 * cd + 8
-            ]
+            at = pl.multiple_of(cd * COVER * TILES + t * COVER, COVER)
+            tile_grad[pl.ds(at, COVER), :] = summed[8 * cd : 8 * cd + 8]
         return carry
 
     lax.fori_loop(0, TILES, scatter_tile, 0, unroll=UNROLL_SCATTER)
 
-    entry_rows = entry_of(cover_rows_ref[...], u)
-    entry_rows = jnp.concatenate([entry_rows[n : n + 1] for n in range(COVER)], axis=1)
+    entry_line = entry_of(cover_line_ref[...], u)
     entry_ids = lax.broadcasted_iota(jnp.int32, (WIN * CAP, TILES * COVER), 0)
-    pick = jnp.where(entry_ids == entry_rows, 1.0, 0.0).astype(BF16)
+    pick = jnp.where(entry_ids == entry_line, 1.0, 0.0).astype(BF16)
     for cd in range(9):
         values = tile_grad[pl.ds(cd * COVER * TILES, COVER * TILES), :]
         high = values.astype(BF16)
@@ -220,7 +233,10 @@
 
 
 def call(kernel, out_shapes, args, scalars=0, scratch=(), name=None):
-    shapes = [jax.ShapeDtypeStruct(s, F32) for s in out_shapes]
+    args = args[:scalars] + tuple(
+        pltpu.with_memory_space_constraint(a, pltpu.VMEM) for a in args[scalars:]
+    )
+    shapes = [pltpu.VMEM(s, F32) for s in out_shapes]
     single = len(shapes) == 1
     return pl.pallas_call(
         kernel,
@@ -236,29 +252,34 @@
     return lax.all_to_all(array, axis, 0, 0, tiled=True)
 
 
-def tile_call(u, fetch_list, tile_cover, table, pix_slot, barycentric, camera, target):
+def tile_call(u, requests, tile_cover, cover_line, table, pix_slot, barycentric, camera, target):
     return call(
         tile_kernel,
         [(WIN, 24, LANES), (8, LANES)],
         (
             u.reshape(1),
-            fetch_list,
-            tile_cover,
-            tile_cover,
+            requests,
+            jnp.transpose(tile_cover),
+            cover_line,
             table,
             pix_slot,
             barycentric,
             camera,
             target,
         ),
-        scalars=3,
+        scalars=1,
         scratch=(
+            pltpu.SMEM((CAP, HOLDERS), jnp.int32),
+            pltpu.SMEM((COVER, TILES), jnp.int32),
+            pltpu.VMEM((COVER, TILES), jnp.int32),
+            pltpu.SemaphoreType.DMA((2,)),
             pltpu.VMEM((2 * TILES, LANES), jnp.int32),
             pltpu.VMEM((16 * WIN, LANES), jnp.int32),
             pltpu.VMEM((8 * WIN * CAP, LANES), F32),
-            pltpu.VMEM((WIN * CAP, LANES), F32),
+            pltpu.VMEM((8 * WIN * CAP, LANES), F32),
             pltpu.VMEM((8 * TILES, LANES), F32),
-            pltpu.VMEM((9 * 2 * TILES, LANES), F32),
+            pltpu.VMEM((8 * 2 * TILES, LANES), F32),
+            pltpu.VMEM((2 * TILES, LANES), F32),
             pltpu.VMEM((18 * 2 * TILES, LANES), F32),
             pltpu.VMEM((9 * TILES * COVER, LANES), F32),
             pltpu.VMEM((9 * WIN * CAP, LANES), F32),
@@ -300,23 +321,30 @@
     )
     shapes = coeffs.shape[0]
     basis = jnp.transpose(shape_basis, (1, 0, 2))
+    rest = rest_pose.reshape(24, LANES)
+    corners = triangles.reshape(3 * BLOCKS, LANES).astype(F32)
+    u, coeffs, rest, corners = lax.optimization_barrier((u, coeffs, rest, corners))
     partial = lax.dot_general(
         coeffs[None], basis, (((1,), (1,)), ((), ())), preferred_element_type=F32
     )
-    rest = rest_pose.reshape(24, LANES)
-    corners = triangles.reshape(3 * BLOCKS, LANES).astype(F32)
-    u, partial, rest, corners = lax.optimization_barrier((u, partial, rest, corners))
+    partial = lax.optimization_barrier(partial)
     positions = rest + to_all(partial.reshape(24, LANES), "view").sum(axis=0)
     shard = along_window(jnp.concatenate([positions, corners], axis=0), -1)
+    cover_line = tile_cover.reshape(1, TILES * COVER)
+    requests = jnp.maximum(jnp.transpose(fetch_list[0]), 0)
+    shard, cover_line, requests, camera = lax.optimization_barrier(
+        (shard, cover_line, requests, camera)
+    )
     table = to_all(shard, "view")
     parts, energy = tile_call(
         u,
-        jnp.transpose(fetch_list[0]),
-        jnp.transpose(tile_cover),
+        requests,
+        tile_cover,
+        cover_line,
         table,
         pix_slot,
         jnp.transpose(barycentric, (1, 0, 2)),
-        jnp.transpose(camera),
+        camera,
         jnp.transpose(target, (1, 0, 2)),
     )
     returned = along_window(exchange(parts, "view").sum(axis=0), 1)
@@ -327,6 +355,7 @@
     energy_part = energy_part[:shapes] + energy_part[shapes:]
     rows = jnp.concatenate([coeff_part, energy_part]).reshape(1, 2 * shapes)
     total = to_all(rows, "vertex").sum(axis=(0, 1))
+    total, vertex_grad = lax.optimization_barrier((total, vertex_grad))
     return (jnp.sum(total[shapes:]) / pixels, vertex_grad, total[:shapes])
 
 

time: 102 us -> 99.5 us (0.975)
  blocking collectives: 66.8 us -> 53.1 us
  waiting for transfers between devices: 11 us -> 17.5 us
  starting transfers between devices: 9.41 us -> 15.5 us
  Pallas kernels: 6.96 us -> 5.19 us
    all_to_all x5 -> x4, blocking collectives: 66.8 us -> 53.1 us  [exchange(): return lax.all_to_all(array, axis, 0, 0, tiled=True)]
    all_to_all x0 -> x1, waiting for transfers between devices: none -> 6.72 us  [exchange(): return lax.all_to_all(array, axis, 0, 0, tiled=True)]
    all_to_all x0 -> x1, starting transfers between devices: none -> 6.32 us  [exchange(): return lax.all_to_all(array, axis, 0, 0, tiled=True)]
    pallas_call x1, Pallas kernels: 6.96 us -> 5.19 us  [call(): pl.pallas_call(kernel, out_shape=shapes[0] if single else shapes, in_spec...]
    unnamed x12 -> x21, local copies, waits for them, and re-layouts: 1.8 us -> 0.55 us
  transfers between devices with their start and end apart: 2 -> 3, of which waited for: 2 -> 3; matrix products, arithmetic and copies ran while one was open for 0% -> 0% of each run, Pallas kernels for 0% -> 0%
where the time goes in v4:
time: 99.5 us; the launch traced here: 98.9 us
  blocking collectives  53.1 us (53%)
  waiting for transfers between devices  17.5 us (18%)
  starting transfers between devices  15.5 us (16%)
  Pallas kernels  5.19 us (5%)
  between operations  2.57 us (3%)
  local copies, waits for them, and re-layouts  2.28 us (2%)
  other arithmetic  1.55 us (2%)
  matrix products  1.16 us (1%)
    all_to_all x4, blocking collectives, exchange(): return lax.all_to_all(array, axis, 0, 0, tiled=True)  53.1 us
    ppermute x2, waiting for transfers between devices, along_window(): return lax.ppermute(array, ('vertex', 'view'), pairs)  10.8 us
    ppermute x2, starting transfers between devices, along_window(): return lax.ppermute(array, ('vertex', 'view'), pairs)  9.22 us
    all_to_all x1, waiting for transfers between devices, exchange(): return lax.all_to_all(array, axis, 0, 0, tiled=True)  6.72 us
    all_to_all x1, starting transfers between devices, exchange(): return lax.all_to_all(array, axis, 0, 0, tiled=True)  6.32 us
    pallas_call x1, Pallas kernels, call(): pl.pallas_call(kernel, out_shape=shapes[0] if single else shapes, in_spec...  5.19 us
  transfers between devices with their start and end apart: 3, of which 3 were waited for; matrix products, arithmetic and copies ran while one was open for 0% of the time, Pallas kernels for 0%

profile of v4, /device:TPU:1, one launch (start us, length us, event | category | flops | bytes accessed | tf_op | source)
XLA Modules:
  0.0 98.9 jit_solution(6839783224006404169)
XLA Ops:
  0.6 0.0 copy-start
  0.6 0.0 copy-start.7
  0.7 0.7 reshape.30
  1.4 0.0 copy-done.7
  1.4 0.0 copy-done
  1.5 1.2 %fusion = f32[1,3,1024]{2,0,1:T(1,128)S(1)} fusion(bf16[64,3,1024]{2,0,1:T(8,128)(2,1)} %param.11, bf16[64]{0:T(256)(128)(2,1)S(1)} %copy-done), kind=kOutput, calls=%fused_computation.1 | convolution fusion | flops 393216 | bytes 405632 | tf_op jit(solution)/shard_map/dot_general | solution.py:327
  2.7 14.2 %all_to_all.25 = f32[8,24,128]{2,1,0:T(8,128)S(1)} all-to-all(f32[8,24,128]{2,1,0:T(8,128)S(1)} %broadcast_in_dim.11), channel_id=1, replica_groups=mesh['vertex'=64,'view'=8] {'view'}, dimensions={0} | all-to-all | bytes 196608 | tf_op jit(solution)/shard_map/all_to_all | solution.py:252
  16.9 0.0 copy-start.9
  16.9 0.0 copy-start.4
  16.9 1.9 %collective-permute-start = (f32[72,128]{1,0:T(8,128)S(1)}, f32[72,128]{1,0:T(8,128)S(1)}, u32[]{:S(2)}, u32[]{:S(2)}) collective-permute-start(f32[72,128]{1,0:T(8,128)S(1)} %pad_maximum_fusion), channel_id=1, source_target_pairs={{0,24},{1,17},{2,10},{3,3},{4,508},{5,501},{6,494},{7,263},{8,32},... | collective-permute-start | bytes 110600 | tf_op jit(solution)/shard_map/ppermute | solution.py:303
  18.8 0.0 copy-done.9
  18.9 0.1 copy.19
  19.0 0.1 reshape.32.cover_line_ref
  19.0 10.0 %collective-permute-done = f32[72,128]{1,0:T(8,128)S(1)} collective-permute-done((f32[72,128]{1,0:T(8,128)S(1)}, f32[72,128]{1,0:T(8,128)S(1)}, u32[]{:S(2)}, u32[]{:S(2)}) %collective-permute-start) | collective-permute-done | bytes 36896 | tf_op jit(solution)/shard_map/ppermute | solution.py:303
  29.0 0.7 broadcast_in_dim.12
  29.7 6.3 %all-to-all-start.1 = ((f32[8,72,128]{2,1,0:T(8,128)}), f32[8,72,128]{2,1,0:T(8,128)S(1)}, u32[]{:S(2)}, u32[]{:S(2)}) async-start(f32[8,72,128]{2,1,0:T(8,128)} %broadcast_in_dim.12), calls=%async_computation.1 | async-start | bytes 589824 | tf_op jit(solution)/shard_map/all_to_all | solution.py:252
  36.1 0.0 copy-done.8
  36.1 0.1 copy.20.camera_ref
  36.1 6.7 %all-to-all-done.1.table_ref = f32[8,72,128]{2,1,0:T(8,128)S(1)} async-done(((f32[8,72,128]{2,1,0:T(8,128)}), f32[8,72,128]{2,1,0:T(8,128)S(1)}, u32[]{:S(2)}, u32[]{:S(2)}) %all-to-all-start.1) | async-done | bytes 294944 | tf_op jit(solution)/shard_map/all_to_all | solution.py:252
  42.9 0.0 copy-done.1
  42.9 5.2 %tiles.1 = (f32[8,24,128]{2,1,0:T(8,128)S(1)}, f32[8,128]{1,0:T(8,128)S(1)}) custom-call(s32[1]{0:T(128)} %bitcast.1.u_ref, s32[4,64]{1,0:T(4,128)S(1)} %maximum_bitcast_fusion.fetch_rows_ref, s32[8,32]{1,0:T(8,128)S(1)} %bitcast.19, s32[1,256]{1,0:T(1,128)S(1)} %reshape.32.cover_line_ref, f32[8,72,128]{2,1,0:T(8,128)S(1)} %all-to-all-done.1.table_ref, ...), custom_call_target="tpu_custom_call" | custom-call | tf_op jit(solution)/shard_map/tiles/pallas_call | solution.py:241
  48.1 8.4 %all_to_all.26 = f32[8,24,128]{2,1,0:T(8,128)S(1)} all-to-all(f32[8,24,128]{2,1,0:T(8,128)S(1)} %get-tuple-element.23), channel_id=1, replica_groups=mesh['vertex'=64,'view'=8] {'view'}, dimensions={0} | all-to-all | bytes 196608 | tf_op jit(solution)/shard_map/all_to_all | solution.py:252
  56.5 7.3 %collective-permute-start.1 = (f32[24,128]{1,0:T(8,128)S(1)}, f32[24,128]{1,0:T(8,128)S(1)}, u32[]{:S(2)}, u32[]{:S(2)}) collective-permute-start(f32[24,128]{1,0:T(8,128)S(1)} %reduce_sum.64), channel_id=1, source_target_pairs={{0,488},{1,497},{2,506},{3,3},{4,12},{5,21},{6,30},{7,263},{8,496}... | collective-permute-start | bytes 36872 | tf_op jit(solution)/shard_map/ppermute | solution.py:303
  63.8 0.8 collective-permute-done.1
  64.7 11.0 %all_to_all.27 = f32[8,32,128]{2,1,0:T(8,128)S(1)} all-to-all(f32[8,32,128]{2,1,0:T(8,128)S(1)} %broadcast_in_dim.13), channel_id=1, replica_groups=mesh['vertex'=64,'view'=8] {'view'}, dimensions={0} | all-to-all | bytes 262144 | tf_op jit(solution)/shard_map/all_to_all | solution.py:252
  75.7 0.1 slice_add_fusion
  75.8 0.0 copy-start.6
  75.8 0.2 multiply_reduce_fusion
  76.0 0.4 copy-done.6
  76.4 0.1 pad_maximum_fusion.2
  76.5 19.5 %all_to_all.28 = f32[64,1,128]{2,1,0:T(1,128)S(1)} all-to-all(f32[64,1,128]{2,1,0:T(1,128)S(1)} %broadcast_in_dim.14), channel_id=1, replica_groups=mesh['vertex'=64,'view'=8] {'vertex'}, dimensions={0} | all-to-all | bytes 65536 | tf_op jit(solution)/shard_map/all_to_all | solution.py:252
  96.0 1.1 %fusion.3 = (f32[64]{0:T(128)}, f32[]{:T(128)}) fusion(f32[128]{0:T(128)S(1)} %reduce_sum.68), kind=kLoop, calls=%fused_computation.11 | loop fusion | flops 63 | bytes 772 | tf_op jit(solution)/shard_map/slice | solution.py:359
  (27 shorter events, 0.2 us)
Async XLA Ops:
  0.6 0.8 copy-start
  0.6 0.8 copy-start.7
  16.9 2.0 %copy-start.9 = (s32[1,64,4]{1,2,0:T(4,128)S(1)}, s32[1,64,4]{1,2,0:T(4,128)}, u32[]{:S(2)}) copy-start(s32[1,64,4]{1,2,0:T(4,128)} %param.14) | copy-start | bytes 3076
  16.9 2.0 %copy-start.4 = (s32[32,8]{0,1:T(8,128)S(1)}, s32[32,8]{0,1:T(8,128)}, u32[]{:S(2)}) copy-start(s32[32,8]{0,1:T(8,128)} %param.15) | copy-start | bytes 3076
  16.9 12.1 %collective-permute-start = (f32[72,128]{1,0:T(8,128)S(1)}, f32[72,128]{1,0:T(8,128)S(1)}, u32[]{:S(2)}, u32[]{:S(2)}) collective-permute-start(f32[72,128]{1,0:T(8,128)S(1)} %pad_maximum_fusion), channel_id=1, source_target_pairs={{0,24},{1,17},{2,10},{3,3},{4,508},{5,501},{6,494},{7,263},{8,32},... | collective-permute-start | bytes 110600 | tf_op jit(solution)/shard_map/ppermute | solution.py:303
  29.7 6.3 %copy-start.8 = (f32[32,12]{0,1:T(8,128)S(1)}, f32[32,12]{0,1:T(8,128)}, u32[]{:S(2)}) copy-start(f32[32,12]{0,1:T(8,128)} %param.18) | copy-start | bytes 4612
  29.7 13.1 %copy-start.1 = (f32[32,3,256]{2,0,1:T(8,128)S(1)}, f32[32,3,256]{2,0,1:T(8,128)}, u32[]{:S(2)}) copy-start(f32[32,3,256]{2,0,1:T(8,128)} %param.17) | copy-start | bytes 294916
  29.7 13.1 %copy-start.2 = (f32[32,3,256]{2,0,1:T(8,128)S(1)}, f32[32,3,256]{2,0,1:T(8,128)}, u32[]{:S(2)}) copy-start(f32[32,3,256]{2,0,1:T(8,128)} %param.19) | copy-start | bytes 294916
  29.7 13.1 %copy-start.3 = (s32[32,256]{1,0:T(8,128)S(1)}, s32[32,256]{1,0:T(8,128)}, u32[]{:S(2)}) copy-start(s32[32,256]{1,0:T(8,128)} %slot_ref.1) | copy-start | bytes 98308
  29.7 13.1 %all-to-all-start.1 = ((f32[8,72,128]{2,1,0:T(8,128)}), f32[8,72,128]{2,1,0:T(8,128)S(1)}, u32[]{:S(2)}, u32[]{:S(2)}) async-start(f32[8,72,128]{2,1,0:T(8,128)} %broadcast_in_dim.12), calls=%async_computation.1 | async-start | bytes 589824 | tf_op jit(solution)/shard_map/all_to_all | solution.py:252
  56.5 19.3 %copy-start.5 = (bf16[64,3,1024]{2,0,1:T(8,128)(2,1)S(1)}, bf16[64,3,1024]{2,0,1:T(8,128)(2,1)}, u32[]{:S(2)}) copy-start(bf16[64,3,1024]{2,0,1:T(8,128)(2,1)} %param.11) | copy-start | bytes 1179652
  56.5 8.1 %collective-permute-start.1 = (f32[24,128]{1,0:T(8,128)S(1)}, f32[24,128]{1,0:T(8,128)S(1)}, u32[]{:S(2)}, u32[]{:S(2)}) collective-permute-start(f32[24,128]{1,0:T(8,128)S(1)} %reduce_sum.64), channel_id=1, source_target_pairs={{0,488},{1,497},{2,506},{3,3},{4,12},{5,21},{6,30},{7,263},{8,496}... | collective-permute-start | bytes 36872 | tf_op jit(solution)/shard_map/ppermute | solution.py:303
  75.8 0.6 copy-start.6

commit v5 on v4

--- a/solution.py
+++ b/solution.py
@@ -29,9 +29,27 @@
     return jnp.take_along_axis(source, lane, axis=1, mode="promise_in_bounds")
 
 
-def high_low(values):
-    high = values.astype(BF16).astype(F32)
-    return jnp.concatenate([high, values - high], axis=0).astype(BF16)
+def offset_kernel(coeff_ref, basis_ref, rest_ref, corner_ref, out_ref, shard_ref):
+    coeffs = jnp.broadcast_to(coeff_ref[...].astype(F32), (16, coeff_ref.shape[1])).astype(BF16)
+    for d in range(3):
+        row = jnp.dot(coeffs, basis_ref[d], preferred_element_type=F32)[0:1]
+        for s in range(8):
+            cols = slice(s * LANES, (s + 1) * LANES)
+            for v in range(VIEWS):
+                out_ref[v, 8 * d + s : 8 * d + s + 1, :] = row[:, cols]
+            shard_ref[8 * d + s : 8 * d + s + 1, :] = rest_ref[d : d + 1, cols]
+    for c in range(3):
+        for b in range(BLOCKS):
+            shard_ref[24 + c * BLOCKS + b : 25 + c * BLOCKS + b, :] = corner_ref[
+                c : c + 1, b * LANES : (b + 1) * LANES
+            ].astype(F32)
+
+
+def finish_kernel(pixels_ref, total_ref, grad_ref, coeff_ref, loss_ref, out_ref):
+    shapes = coeff_ref.shape[1]
+    coeff_ref[...] = total_ref[:, :shapes]
+    loss_ref[...] = jnp.sum(total_ref[:, shapes:], axis=1, keepdims=True) * pixels_ref[0]
+    out_ref[...] = grad_ref[...]
 
 
 def lane_onehot(lane_row, ids):
@@ -142,7 +160,7 @@
 
     lax.fori_loop(0, TILES, gather_tile, 0, unroll=UNROLL_GATHER)
 
-    camera = camera_ref[...]
+    camera = camera_ref[...].T
     energy = jnp.zeros((TILES, LANES), F32)
     for half in range(2):
         cols = slice(half * LANES, (half + 1) * LANES)
@@ -213,36 +231,39 @@
         both = jnp.dot(
             pick, jnp.concatenate([high, low], axis=1), preferred_element_type=F32
         )
-        entry_grad[pl.ds(cd * WIN * CAP, WIN * CAP), :] = both[:, :LANES] + both[:, LANES:]
+        both = both[:, :LANES] + both[:, LANES:]
+        high = both.astype(BF16).astype(F32)
+        entry_grad[pl.ds(cd * WIN * CAP, WIN * CAP), :] = high
+        entry_grad[pl.ds((9 + cd) * WIN * CAP, WIN * CAP), :] = both - high
 
     for j in range(WIN):
-        rows = [[] for _ in range(3)]
+        rows = [[] for _ in range(6)]
         onehot = []
         for c in range(3):
             for s in range(CAP):
                 ids = corner_id[pl.ds(j * 16 + c * CAP + s, 1), :]
                 mine = jnp.broadcast_to(ids >> 7, (8, LANES)) == sub8
                 onehot.append(lane_onehot(ids & (LANES - 1), ids16))
-                for d in range(3):
-                    at = (3 * c + d) * WIN * CAP + j * CAP + s
+                for d in range(6):
+                    at = (9 * (d // 3) + 3 * c + d % 3) * WIN * CAP + j * CAP + s
                     grad = jnp.broadcast_to(entry_grad[pl.ds(at, 1), :], (8, LANES))
                     rows[d].append(jnp.where(mine, grad, 0.0))
         stacked = jnp.concatenate([jnp.concatenate(r, axis=1) for r in rows], axis=0)
-        summed = dot_nt(high_low(stacked), jnp.concatenate(onehot, axis=1))
+        summed = dot_nt(stacked.astype(BF16), jnp.concatenate(onehot, axis=1))
         out_ref[j] = summed[:24] + summed[24:]
 
 
-def call(kernel, out_shapes, args, scalars=0, scratch=(), name=None):
-    args = args[:scalars] + tuple(
-        pltpu.with_memory_space_constraint(a, pltpu.VMEM) for a in args[scalars:]
-    )
-    shapes = [pltpu.VMEM(s, F32) for s in out_shapes]
-    single = len(shapes) == 1
+def call(kernel, out_shapes, args, scalars=0, scratch=(), name=None, pinned=(True, True)):
+    if pinned[0]:
+        args = args[:scalars] + tuple(
+            pltpu.with_memory_space_constraint(a, pltpu.VMEM) for a in args[scalars:]
+        )
+    kind = pltpu.VMEM if pinned[1] else jax.ShapeDtypeStruct
     return pl.pallas_call(
         kernel,
-        out_shape=shapes[0] if single else shapes,
+        out_shape=[kind(s, F32) for s in out_shapes],
         in_specs=[SMEM] * scalars + [VMEM] * (len(args) - scalars),
-        out_specs=VMEM if single else [VMEM] * len(shapes),
+        out_specs=[VMEM] * len(out_shapes),
         scratch_shapes=list(scratch),
         name=name,
     )(*args)
@@ -282,7 +303,7 @@
             pltpu.VMEM((2 * TILES, LANES), F32),
             pltpu.VMEM((18 * 2 * TILES, LANES), F32),
             pltpu.VMEM((9 * TILES * COVER, LANES), F32),
-            pltpu.VMEM((9 * WIN * CAP, LANES), F32),
+            pltpu.VMEM((18 * WIN * CAP, LANES), F32),
         ),
         name="tiles",
     )
@@ -321,19 +342,21 @@
     )
     shapes = coeffs.shape[0]
     basis = jnp.transpose(shape_basis, (1, 0, 2))
-    rest = rest_pose.reshape(24, LANES)
-    corners = triangles.reshape(3 * BLOCKS, LANES).astype(F32)
-    u, coeffs, rest, corners = lax.optimization_barrier((u, coeffs, rest, corners))
-    partial = lax.dot_general(
-        coeffs[None], basis, (((1,), (1,)), ((), ())), preferred_element_type=F32
-    )
-    partial = lax.optimization_barrier(partial)
-    positions = rest + to_all(partial.reshape(24, LANES), "view").sum(axis=0)
-    shard = along_window(jnp.concatenate([positions, corners], axis=0), -1)
+    partial, shard = call(
+        offset_kernel,
+        [(VIEWS, 24, LANES), (SHARD, LANES)],
+        (coeffs.reshape(1, shapes), basis, rest_pose, triangles),
+        name="offsets",
+        pinned=(False, True),
+    )
+    offsets = exchange(partial, "view").sum(axis=0)
+    shard = shard + jnp.pad(offsets, ((0, SHARD - 24), (0, 0)))
+    shard = along_window(shard, -1)
     cover_line = tile_cover.reshape(1, TILES * COVER)
     requests = jnp.maximum(jnp.transpose(fetch_list[0]), 0)
-    shard, cover_line, requests, camera = lax.optimization_barrier(
-        (shard, cover_line, requests, camera)
+    lens = jnp.pad(jnp.transpose(camera), ((0, 4), (0, 0)))
+    shard, cover_line, requests, lens, u = lax.optimization_barrier(
+        (shard, cover_line, requests, lens, u)
     )
     table = to_all(shard, "view")
     parts, energy = tile_call(
@@ -344,7 +367,7 @@
         table,
         pix_slot,
         jnp.transpose(barycentric, (1, 0, 2)),
-        camera,
+        lens,
         jnp.transpose(target, (1, 0, 2)),
     )
     returned = along_window(exchange(parts, "view").sum(axis=0), 1)
@@ -354,9 +377,16 @@
     energy_part = total[24:].sum(axis=0)
     energy_part = energy_part[:shapes] + energy_part[shapes:]
     rows = jnp.concatenate([coeff_part, energy_part]).reshape(1, 2 * shapes)
-    total = to_all(rows, "vertex").sum(axis=(0, 1))
-    total, vertex_grad = lax.optimization_barrier((total, vertex_grad))
-    return (jnp.sum(total[shapes:]) / pixels, vertex_grad, total[:shapes])
+    total = to_all(rows, "vertex").sum(axis=0)
+    coeff_grad, loss, vertex_grad = call(
+        finish_kernel,
+        [(1, shapes), (1, 1), vertex_grad.shape],
+        (jnp.full((1,), 1.0 / pixels, F32), total, vertex_grad),
+        scalars=1,
+        name="finish",
+        pinned=(True, False),
+    )
+    return (loss.reshape(()), vertex_grad, coeff_grad.reshape(shapes))
 
 
 def solution(mesh):

time: 99.5 us -> 95 us (0.955)
  blocking collectives: 53.1 us -> 65.2 us
  waiting for transfers between devices: 17.5 us -> 10.1 us
  starting transfers between devices: 15.5 us -> 9.99 us
  Pallas kernels: 5.19 us -> 7.11 us
  between operations: 2.57 us -> 0.79 us
  local copies, waits for them, and re-layouts: 2.28 us -> 0.94 us
  matrix products: 1.16 us -> 0 us
  other arithmetic: 1.55 us -> 0.42 us
    all_to_all x4 -> x5, blocking collectives: 53.1 us -> 65.2 us  [exchange(): return lax.all_to_all(array, axis, 0, 0, tiled=True)]
    all_to_all x1 -> x0, waiting for transfers between devices: 6.72 us -> none  [exchange(): return lax.all_to_all(array, axis, 0, 0, tiled=True)]
    all_to_all x1 -> x0, starting transfers between devices: 6.32 us -> none  [exchange(): return lax.all_to_all(array, axis, 0, 0, tiled=True)]
    pallas_call x1 -> x3, Pallas kernels: 5.19 us -> 7.11 us  [call(): pl.pallas_call(kernel, out_shape=[kind(s, F32) for s in out_shapes], in_s...]
    dot_general x1 -> x0, matrix products: 1.16 us -> none  [per_device(): lax.dot_general(coeffs[None], basis, (((1,), (1,)), ((), ())), preferred_...]
    slice x1 -> x0, other arithmetic: 1.11 us -> none  [per_device(): return (jnp.sum(total[shapes:]) / pixels, vertex_grad, total[:shapes])]
  transfers between devices with their start and end apart: 3 -> 2, of which waited for: 3 -> 2; matrix products, arithmetic and copies ran while one was open for 0% -> 0% of each run, Pallas kernels for 0% -> 0%
where the time goes in v5:
time: 95 us; the launch traced here: 94.6 us
  blocking collectives  65.2 us (69%)
  waiting for transfers between devices  10.1 us (11%)
  starting transfers between devices  9.99 us (11%)
  Pallas kernels  7.11 us (7%)
    all_to_all x5, blocking collectives, exchange(): return lax.all_to_all(array, axis, 0, 0, tiled=True)  65.2 us
    ppermute x2, waiting for transfers between devices, along_window(): return lax.ppermute(array, ('vertex', 'view'), pairs)  10.1 us
    ppermute x2, starting transfers between devices, along_window(): return lax.ppermute(array, ('vertex', 'view'), pairs)  9.99 us
    pallas_call x3, Pallas kernels, call(): pl.pallas_call(kernel, out_shape=[kind(s, F32) for s in out_shapes], in_s...  7.11 us
  transfers between devices with their start and end apart: 2, of which 2 were waited for; matrix products, arithmetic and copies ran while one was open for 0% of the time, Pallas kernels for 0%

profile of v5, /device:TPU:1, one launch (start us, length us, event | category | flops | bytes accessed | tf_op | source)
XLA Modules:
  0.0 94.6 jit_solution(1493963153810540281)
XLA Ops:
  0.6 1.2 %offsets.1 = (f32[8,24,128]{2,1,0:T(8,128)S(1)}, f32[72,128]{1,0:T(8,128)S(1)}) custom-call(bf16[1,64]{1,0:T(2,128)(2,1)} %bitcast.23, bf16[3,64,1024]{2,1,0:T(8,128)(2,1)} %bitcast.20, f32[3,1024]{1,0:T(4,128)} %rest_ref.1, s32[3,2048]{1,0:T(4,128)} %corner_ref.1), custom_call_target="tpu_custom_call" | custom-call | tf_op jit(solution)/shard_map/offsets/pallas_call | solution.py:262
  1.8 14.2 %all_to_all.25 = f32[8,24,128]{2,1,0:T(8,128)S(1)} all-to-all(f32[8,24,128]{2,1,0:T(8,128)S(1)} %get-tuple-element.16), channel_id=1, replica_groups=mesh['vertex'=64,'view'=8] {'view'}, dimensions={0} | all-to-all | bytes 196608 | tf_op jit(solution)/shard_map/all_to_all | solution.py:273
  16.1 0.0 copy-start.6
  16.1 0.0 copy-start.5
  16.1 1.9 %collective-permute-start = (f32[72,128]{1,0:T(8,128)S(1)}, f32[72,128]{1,0:T(8,128)S(1)}, u32[]{:S(2)}, u32[]{:S(2)}) collective-permute-start(f32[72,128]{1,0:T(8,128)S(1)} %pad_add_fusion), channel_id=1, source_target_pairs={{0,24},{1,17},{2,10},{3,3},{4,508},{5,501},{6,494},{7,263},{8,32},... | collective-permute-start | bytes 110600 | tf_op jit(solution)/shard_map/ppermute | solution.py:324
  18.0 0.0 copy-done.6
  18.0 0.0 copy-done.5
  18.1 0.0 copy-start.3
  18.1 0.7 copy-done.3
  18.7 0.1 copy.16
  18.8 0.1 reshape.32.cover_line_ref
  18.9 9.3 %collective-permute-done = f32[72,128]{1,0:T(8,128)S(1)} collective-permute-done((f32[72,128]{1,0:T(8,128)S(1)}, f32[72,128]{1,0:T(8,128)S(1)}, u32[]{:S(2)}, u32[]{:S(2)}) %collective-permute-start) | collective-permute-done | bytes 36896 | tf_op jit(solution)/shard_map/ppermute | solution.py:324
  28.2 0.0 copy-start
  28.2 0.0 copy-start.1
  28.2 0.0 copy-start.2
  28.2 12.6 %all_to_all.26.table_ref = f32[8,72,128]{2,1,0:T(8,128)S(1)} all-to-all(f32[8,72,128]{2,1,0:T(8,128)S(1)} %broadcast_in_dim.6), channel_id=1, replica_groups=mesh['vertex'=64,'view'=8] {'view'}, dimensions={0} | all-to-all | bytes 589824 | tf_op jit(solution)/shard_map/all_to_all | solution.py:273
  40.9 0.0 copy-done
  40.9 0.0 copy-done.1
  40.9 0.0 copy-done.2
  40.9 5.1 %tiles.1 = (f32[8,24,128]{2,1,0:T(8,128)S(1)}, f32[8,128]{1,0:T(8,128)S(1)}) custom-call(s32[1]{0:T(128)} %bitcast.5.u_ref, s32[4,64]{1,0:T(4,128)S(1)} %maximum_bitcast_fusion.fetch_rows_ref, s32[8,32]{1,0:T(8,128)S(1)} %bitcast.18, s32[1,256]{1,0:T(1,128)S(1)} %reshape.32.cover_line_ref, f32[8,72,128]{2,1,0:T(8,128)S(1)} %all_to_all.26.table_ref, ...), custom_call_target="tpu_custom_call" | custom-call | tf_op jit(solution)/shard_map/tiles/pallas_call | solution.py:262
  46.1 7.9 %all_to_all.27 = f32[8,24,128]{2,1,0:T(8,128)S(1)} all-to-all(f32[8,24,128]{2,1,0:T(8,128)S(1)} %get-tuple-element.22), channel_id=1, replica_groups=mesh['vertex'=64,'view'=8] {'view'}, dimensions={0} | all-to-all | bytes 196608 | tf_op jit(solution)/shard_map/all_to_all | solution.py:273
  54.0 0.0 copy-start.4
  54.0 8.1 %collective-permute-start.1 = (f32[24,128]{1,0:T(8,128)S(1)}, f32[24,128]{1,0:T(8,128)S(1)}, u32[]{:S(2)}, u32[]{:S(2)}) collective-permute-start(f32[24,128]{1,0:T(8,128)S(1)} %reduce_sum.57), channel_id=1, source_target_pairs={{0,488},{1,497},{2,506},{3,3},{4,12},{5,21},{6,30},{7,263},{8,496}... | collective-permute-start | bytes 36872 | tf_op jit(solution)/shard_map/ppermute | solution.py:324
  62.1 0.8 collective-permute-done.1
  62.9 10.5 %all_to_all.28 = f32[8,32,128]{2,1,0:T(8,128)S(1)} all-to-all(f32[8,32,128]{2,1,0:T(8,128)S(1)} %broadcast_in_dim.7), channel_id=1, replica_groups=mesh['vertex'=64,'view'=8] {'view'}, dimensions={0} | all-to-all | bytes 262144 | tf_op jit(solution)/shard_map/all_to_all | solution.py:273
  73.4 0.1 slice_add_fusion
  73.5 0.0 copy-done.4
  73.5 0.2 multiply_reduce_fusion
  73.7 0.1 pad_maximum_fusion.1
  73.8 20.0 %all_to_all.29 = f32[64,1,128]{2,1,0:T(1,128)S(1)} all-to-all(f32[64,1,128]{2,1,0:T(1,128)S(1)} %broadcast_in_dim.8), channel_id=1, replica_groups=mesh['vertex'=64,'view'=8] {'vertex'}, dimensions={0} | all-to-all | bytes 65536 | tf_op jit(solution)/shard_map/all_to_all | solution.py:273
  93.8 0.8 finish.1
  (14 shorter events, 0.2 us)
Async XLA Ops:
  16.1 2.0 %copy-start.6 = (s32[1,64,4]{1,2,0:T(4,128)S(1)}, s32[1,64,4]{1,2,0:T(4,128)}, u32[]{:S(2)}) copy-start(s32[1,64,4]{1,2,0:T(4,128)} %param.14) | copy-start | bytes 3076
  16.1 2.0 %copy-start.5 = (f32[32,12]{0,1:T(8,128)S(1)}, f32[32,12]{0,1:T(8,128)}, u32[]{:S(2)}) copy-start(f32[32,12]{0,1:T(8,128)} %param.18) | copy-start | bytes 4612
  16.1 12.1 %collective-permute-start = (f32[72,128]{1,0:T(8,128)S(1)}, f32[72,128]{1,0:T(8,128)S(1)}, u32[]{:S(2)}, u32[]{:S(2)}) collective-permute-start(f32[72,128]{1,0:T(8,128)S(1)} %pad_add_fusion), channel_id=1, source_target_pairs={{0,24},{1,17},{2,10},{3,3},{4,508},{5,501},{6,494},{7,263},{8,32},... | collective-permute-start | bytes 110600 | tf_op jit(solution)/shard_map/ppermute | solution.py:324
  18.1 0.7 copy-start.3
  28.2 12.7 %copy-start = (f32[32,3,256]{2,0,1:T(8,128)S(1)}, f32[32,3,256]{2,0,1:T(8,128)}, u32[]{:S(2)}) copy-start(f32[32,3,256]{2,0,1:T(8,128)} %param.17) | copy-start | bytes 294916
  28.2 12.7 %copy-start.1 = (f32[32,3,256]{2,0,1:T(8,128)S(1)}, f32[32,3,256]{2,0,1:T(8,128)}, u32[]{:S(2)}) copy-start(f32[32,3,256]{2,0,1:T(8,128)} %param.19) | copy-start | bytes 294916
  28.2 12.7 %copy-start.2 = (s32[32,256]{1,0:T(8,128)S(1)}, s32[32,256]{1,0:T(8,128)}, u32[]{:S(2)}) copy-start(s32[32,256]{1,0:T(8,128)} %slot_ref.1) | copy-start | bytes 98308
  54.0 19.5 %copy-start.4 = (bf16[64,3,1024]{2,0,1:T(8,128)(2,1)S(1)}, bf16[64,3,1024]{2,0,1:T(8,128)(2,1)}, u32[]{:S(2)}) copy-start(bf16[64,3,1024]{2,0,1:T(8,128)(2,1)} %param.11) | copy-start | bytes 1179652
  54.0 8.9 %collective-permute-start.1 = (f32[24,128]{1,0:T(8,128)S(1)}, f32[24,128]{1,0:T(8,128)S(1)}, u32[]{:S(2)}, u32[]{:S(2)}) collective-permute-start(f32[24,128]{1,0:T(8,128)S(1)} %reduce_sum.57), channel_id=1, source_target_pairs={{0,488},{1,497},{2,506},{3,3},{4,12},{5,21},{6,30},{7,263},{8,496}... | collective-permute-start | bytes 36872 | tf_op jit(solution)/shard_map/ppermute | solution.py:324

commit v6 on v5

--- a/solution.py
+++ b/solution.py
@@ -17,6 +17,7 @@
 COVER = 8
 TILES = 32
 BLOCKS = 16
+PACKED = 40
 SHARD = 24 + 3 * BLOCKS
 
 F32 = jnp.float32
@@ -29,7 +30,16 @@
     return jnp.take_along_axis(source, lane, axis=1, mode="promise_in_bounds")
 
 
-def offset_kernel(coeff_ref, basis_ref, rest_ref, corner_ref, out_ref, shard_ref):
+def offset_kernel(
+    u_ref, coeff_ref, basis_ref, rest_ref, corner_ref, fetch_ref, out_ref, shard_ref
+):
+    requests = jnp.maximum(fetch_ref[...], 0).astype(F32)
+    holder = lax.broadcasted_iota(jnp.int32, requests.shape, 1)
+    for v in range(VIEWS):
+        mine = holder == ((u_ref[0] + OFFSETS[v]) & (HOLDERS - 1))
+        wanted = jnp.sum(jnp.where(mine, requests, 0.0), axis=1, keepdims=True)
+        out_ref[v, 24:28, :] = jnp.broadcast_to(wanted, (CAP, LANES))
+        out_ref[v, 28:32, :] = jnp.zeros((CAP, LANES), F32)
     coeffs = jnp.broadcast_to(coeff_ref[...].astype(F32), (16, coeff_ref.shape[1])).astype(BF16)
     for d in range(3):
         row = jnp.dot(coeffs, basis_ref[d], preferred_element_type=F32)[0:1]
@@ -45,6 +55,24 @@
             ].astype(F32)
 
 
+def pack_kernel(shard_ref, parts_ref, out_ref):
+    wanted = jnp.concatenate([parts_ref[v, 24:28, :BLOCKS] for v in range(VIEWS)], axis=0)
+    ids = lax.broadcasted_iota(jnp.int32, wanted.shape, 1)
+    pick = jnp.where(wanted.astype(jnp.int32) == ids, 1.0, 0.0)
+    for v in range(VIEWS):
+        out_ref[v, 0:24, :] = shard_ref[0:24, :]
+        out_ref[v, 36:40, :] = jnp.zeros((CAP, LANES), F32)
+    for c in range(3):
+        rows = jnp.dot(
+            pick,
+            shard_ref[24 + c * BLOCKS : 24 + (c + 1) * BLOCKS, :],
+            precision=lax.Precision.HIGHEST,
+            preferred_element_type=F32,
+        )
+        for v in range(VIEWS):
+            out_ref[v, 24 + c * CAP : 24 + (c + 1) * CAP, :] = rows[v * CAP : (v + 1) * CAP]
+
+
 def finish_kernel(pixels_ref, total_ref, grad_ref, coeff_ref, loss_ref, out_ref):
     shapes = coeff_ref.shape[1]
     coeff_ref[...] = total_ref[:, :shapes]
@@ -70,7 +98,6 @@
 
 def tile_kernel(
     u_ref,
-    fetch_rows_ref,
     cover_rows_ref,
     cover_line_ref,
     table_ref,
@@ -80,7 +107,6 @@
     target_ref,
     out_ref,
     energy_ref,
-    fetch_ref,
     entry_ref,
     entry_rows,
     sems,
@@ -96,10 +122,8 @@
     entry_grad,
 ):
     u = u_ref[0]
-    fetch_copy = pltpu.make_async_copy(fetch_rows_ref, fetch_ref, sems.at[0])
-    fetch_copy.start()
     entry_rows[...] = entry_of(cover_rows_ref[...], u) * 8
-    entry_copy = pltpu.make_async_copy(entry_rows, entry_ref, sems.at[1])
+    entry_copy = pltpu.make_async_copy(entry_rows, entry_ref, sems.at[0])
     entry_copy.start()
     sub8 = lax.broadcasted_iota(jnp.int32, (8, LANES), 0)
     sub16 = lax.broadcasted_iota(jnp.int32, (16, LANES), 0)
@@ -108,13 +132,8 @@
         slot_rows[half * TILES : (half + 1) * TILES, :] = slot_ref[
             :, half * LANES : (half + 1) * LANES
         ]
-    fetch_copy.wait()
     for j in range(WIN):
-        for s in range(CAP):
-            block = fetch_ref[s, (u + OFFSETS[j]) & (HOLDERS - 1)]
-            for c in range(3):
-                ids = table_ref[j, pl.ds(24 + c * BLOCKS + block, 1), :]
-                corner_id[pl.ds(j * 16 + c * CAP + s, 1), :] = ids.astype(jnp.int32)
+        corner_id[j * 16 : j * 16 + 16, :] = table_ref[j, 24:40, :].astype(jnp.int32)
     for j in range(WIN):
         ids = [corner_id[pl.ds(j * 16 + 8 * i, 8), :] for i in range(2)]
         lane = [i & (LANES - 1) for i in ids]
@@ -273,13 +292,12 @@
     return lax.all_to_all(array, axis, 0, 0, tiled=True)
 
 
-def tile_call(u, requests, tile_cover, cover_line, table, pix_slot, barycentric, camera, target):
+def tile_call(u, tile_cover, cover_line, table, pix_slot, barycentric, camera, target):
     return call(
         tile_kernel,
         [(WIN, 24, LANES), (8, LANES)],
         (
             u.reshape(1),
-            requests,
             jnp.transpose(tile_cover),
             cover_line,
             table,
@@ -290,10 +308,9 @@
         ),
         scalars=1,
         scratch=(
-            pltpu.SMEM((CAP, HOLDERS), jnp.int32),
             pltpu.SMEM((COVER, TILES), jnp.int32),
             pltpu.VMEM((COVER, TILES), jnp.int32),
-            pltpu.SemaphoreType.DMA((2,)),
+            pltpu.SemaphoreType.DMA((1,)),
             pltpu.VMEM((2 * TILES, LANES), jnp.int32),
             pltpu.VMEM((16 * WIN, LANES), jnp.int32),
             pltpu.VMEM((8 * WIN * CAP, LANES), F32),
@@ -344,24 +361,30 @@
     basis = jnp.transpose(shape_basis, (1, 0, 2))
     partial, shard = call(
         offset_kernel,
-        [(VIEWS, 24, LANES), (SHARD, LANES)],
-        (coeffs.reshape(1, shapes), basis, rest_pose, triangles),
+        [(VIEWS, 32, LANES), (SHARD, LANES)],
+        (
+            u.reshape(1),
+            coeffs.reshape(1, shapes),
+            basis,
+            rest_pose,
+            triangles,
+            jnp.transpose(fetch_list[0]),
+        ),
+        scalars=1,
         name="offsets",
         pinned=(False, True),
     )
-    offsets = exchange(partial, "view").sum(axis=0)
+    parts = exchange(partial, "view")
+    offsets = parts[:, :24].sum(axis=0)
     shard = shard + jnp.pad(offsets, ((0, SHARD - 24), (0, 0)))
     shard = along_window(shard, -1)
     cover_line = tile_cover.reshape(1, TILES * COVER)
-    requests = jnp.maximum(jnp.transpose(fetch_list[0]), 0)
     lens = jnp.pad(jnp.transpose(camera), ((0, 4), (0, 0)))
-    shard, cover_line, requests, lens, u = lax.optimization_barrier(
-        (shard, cover_line, requests, lens, u)
-    )
-    table = to_all(shard, "view")
-    parts, energy = tile_call(
+    shard, cover_line, lens, u = lax.optimization_barrier((shard, cover_line, lens, u))
+    packed = call(pack_kernel, [(VIEWS, PACKED, LANES)], (shard, parts), name="pack")[0]
+    table = exchange(packed, "view")
+    grads, energy = tile_call(
         u,
-        requests,
         tile_cover,
         cover_line,
         table,
@@ -370,7 +393,7 @@
         lens,
         jnp.transpose(target, (1, 0, 2)),
     )
-    returned = along_window(exchange(parts, "view").sum(axis=0), 1)
+    returned = along_window(exchange(grads, "view").sum(axis=0), 1)
     total = to_all(jnp.concatenate([returned, energy], axis=0), "view").sum(axis=0)
     vertex_grad = total[:24].reshape(3, VIEWS * LANES)
     coeff_part = jnp.sum(basis.astype(F32) * vertex_grad[:, None, :], axis=(0, 2))

time: 95 us -> 94 us (0.989)
  blocking collectives: 65.2 us -> 64.2 us
    all_to_all x5, blocking collectives: 65.2 us -> 64.2 us  [exchange(): return lax.all_to_all(array, axis, 0, 0, tiled=True)]
    pallas_call x3 -> x4, Pallas kernels: 7.11 us -> 7.2 us  [call(): pl.pallas_call(kernel, out_shape=[kind(s, F32) for s in out_shapes], in_s...]
where the time goes in v6:
time: 94 us; the launch traced here: 93.5 us
  blocking collectives  64.2 us (68%)
  waiting for transfers between devices  10.2 us (11%)
  starting transfers between devices  9.98 us (11%)
  Pallas kernels  7.2 us (8%)
    all_to_all x5, blocking collectives, exchange(): return lax.all_to_all(array, axis, 0, 0, tiled=True)  64.2 us
    ppermute x2, waiting for transfers between devices, along_window(): return lax.ppermute(array, ('vertex', 'view'), pairs)  10.2 us
    ppermute x2, starting transfers between devices, along_window(): return lax.ppermute(array, ('vertex', 'view'), pairs)  9.98 us
    pallas_call x4, Pallas kernels, call(): pl.pallas_call(kernel, out_shape=[kind(s, F32) for s in out_shapes], in_s...  7.2 us
  transfers between devices with their start and end apart: 2, of which 2 were waited for; matrix products, arithmetic and copies ran while one was open for 0% of the time, Pallas kernels for 0%

profile of v6, /device:TPU:1, one launch (start us, length us, event | category | flops | bytes accessed | tf_op | source)
XLA Modules:
  0.0 93.5 jit_solution(9067655868507446538)
XLA Ops:
  0.6 1.2 %offsets.1 = (f32[8,32,128]{2,1,0:T(8,128)S(1)}, f32[72,128]{1,0:T(8,128)S(1)}) custom-call(s32[1]{0:T(128)} %bitcast.1.u_ref, bf16[1,64]{1,0:T(2,128)(2,1)} %bitcast.24, bf16[3,64,1024]{2,1,0:T(8,128)(2,1)} %bitcast.20, f32[3,1024]{1,0:T(4,128)} %rest_ref.1, s32[3,2048]{1,0:T(4,128)} %corner_ref.1, s32[4,64]{1,0:T(4,128)} %bitcast.23), custom_call_target="tpu_custom_call" | custom-call | tf_op jit(solution)/shard_map/offsets/pallas_call | solution.py:281
  1.8 14.5 %all_to_all.25.parts_ref = f32[8,32,128]{2,1,0:T(8,128)S(1)} all-to-all(f32[8,32,128]{2,1,0:T(8,128)S(1)} %get-tuple-element.15), channel_id=1, replica_groups=mesh['vertex'=64,'view'=8] {'view'}, dimensions={0} | all-to-all | bytes 262144 | tf_op jit(solution)/shard_map/all_to_all | solution.py:292
  16.3 0.0 copy-start.3
  16.3 1.9 %collective-permute-start = (f32[72,128]{1,0:T(8,128)S(1)}, f32[72,128]{1,0:T(8,128)S(1)}, u32[]{:S(2)}, u32[]{:S(2)}) collective-permute-start(f32[72,128]{1,0:T(8,128)S(1)} %pad_add_fusion), channel_id=1, source_target_pairs={{0,24},{1,17},{2,10},{3,3},{4,508},{5,501},{6,494},{7,263},{8,32},... | collective-permute-start | bytes 110600 | tf_op jit(solution)/shard_map/ppermute | solution.py:341
  18.3 0.0 copy-done.3
  18.3 0.1 copy.16
  18.4 0.0 copy-start.5
  18.4 0.1 reshape.33.cover_line_ref
  18.5 0.6 copy-done.5
  19.1 9.4 %collective-permute-done.shard_ref = f32[72,128]{1,0:T(8,128)S(1)} collective-permute-done((f32[72,128]{1,0:T(8,128)S(1)}, f32[72,128]{1,0:T(8,128)S(1)}, u32[]{:S(2)}, u32[]{:S(2)}) %collective-permute-start) | collective-permute-done | bytes 36896 | tf_op jit(solution)/shard_map/ppermute | solution.py:341
  28.4 0.2 pack.1
  28.6 0.0 copy-start
  28.6 0.0 copy-start.1
  28.6 0.0 copy-start.2
  28.6 11.0 %all_to_all.26.table_ref = f32[8,40,128]{2,1,0:T(8,128)S(1)} all-to-all(f32[8,40,128]{2,1,0:T(8,128)S(1)} %pack.1), channel_id=1, replica_groups=mesh['vertex'=64,'view'=8] {'view'}, dimensions={0} | all-to-all | bytes 327680 | tf_op jit(solution)/shard_map/all_to_all | solution.py:292
  39.6 0.0 copy-done
  39.6 0.0 copy-done.1
  39.6 0.0 copy-done.2
  39.6 5.1 %tiles.1 = (f32[8,24,128]{2,1,0:T(8,128)S(1)}, f32[8,128]{1,0:T(8,128)S(1)}) custom-call(s32[1]{0:T(128)} %bitcast.6.u_ref, s32[8,32]{1,0:T(8,128)S(1)} %bitcast.18, s32[1,256]{1,0:T(1,128)S(1)} %reshape.33.cover_line_ref, f32[8,40,128]{2,1,0:T(8,128)S(1)} %all_to_all.26.table_ref, s32[32,256]{1,0:T(8,128)S(1)} %copy-done.2, f32[3,32,256]{2,1,0:T(8,128)S(1)} %bitcast.16, ...), custom_call_target="tpu_custom_call" | custom-call | tf_op jit(solution)/shard_map/tiles/pallas_call | solution.py:281
  44.7 8.3 %all_to_all.27 = f32[8,24,128]{2,1,0:T(8,128)S(1)} all-to-all(f32[8,24,128]{2,1,0:T(8,128)S(1)} %get-tuple-element.20), channel_id=1, replica_groups=mesh['vertex'=64,'view'=8] {'view'}, dimensions={0} | all-to-all | bytes 196608 | tf_op jit(solution)/shard_map/all_to_all | solution.py:292
  52.9 0.0 copy-start.4
  53.0 8.1 %collective-permute-start.1 = (f32[24,128]{1,0:T(8,128)S(1)}, f32[24,128]{1,0:T(8,128)S(1)}, u32[]{:S(2)}, u32[]{:S(2)}) collective-permute-start(f32[24,128]{1,0:T(8,128)S(1)} %reduce_sum.57), channel_id=1, source_target_pairs={{0,488},{1,497},{2,506},{3,3},{4,12},{5,21},{6,30},{7,263},{8,496}... | collective-permute-start | bytes 36872 | tf_op jit(solution)/shard_map/ppermute | solution.py:341
  61.0 0.8 collective-permute-done.1
  61.8 10.5 %all_to_all.28 = f32[8,32,128]{2,1,0:T(8,128)S(1)} all-to-all(f32[8,32,128]{2,1,0:T(8,128)S(1)} %broadcast_in_dim.4), channel_id=1, replica_groups=mesh['vertex'=64,'view'=8] {'view'}, dimensions={0} | all-to-all | bytes 262144 | tf_op jit(solution)/shard_map/all_to_all | solution.py:292
  72.4 0.1 slice_add_fusion
  72.5 0.0 copy-done.4
  72.5 0.2 multiply_reduce_fusion
  72.7 0.1 pad_maximum_fusion.1
  72.8 20.0 %all_to_all.29 = f32[64,1,128]{2,1,0:T(1,128)S(1)} all-to-all(f32[64,1,128]{2,1,0:T(1,128)S(1)} %broadcast_in_dim.5), channel_id=1, replica_groups=mesh['vertex'=64,'view'=8] {'vertex'}, dimensions={0} | all-to-all | bytes 65536 | tf_op jit(solution)/shard_map/all_to_all | solution.py:292
  92.8 0.8 finish.1
  (12 shorter events, 0.1 us)
Async XLA Ops:
  16.3 2.0 %copy-start.3 = (s32[32,8]{0,1:T(8,128)S(1)}, s32[32,8]{0,1:T(8,128)}, u32[]{:S(2)}) copy-start(s32[32,8]{0,1:T(8,128)} %param.15) | copy-start | bytes 3076
  16.3 12.1 %collective-permute-start = (f32[72,128]{1,0:T(8,128)S(1)}, f32[72,128]{1,0:T(8,128)S(1)}, u32[]{:S(2)}, u32[]{:S(2)}) collective-permute-start(f32[72,128]{1,0:T(8,128)S(1)} %pad_add_fusion), channel_id=1, source_target_pairs={{0,24},{1,17},{2,10},{3,3},{4,508},{5,501},{6,494},{7,263},{8,32},... | collective-permute-start | bytes 110600 | tf_op jit(solution)/shard_map/ppermute | solution.py:341
  18.4 0.7 copy-start.5
  28.6 11.0 %copy-start = (f32[32,3,256]{2,0,1:T(8,128)S(1)}, f32[32,3,256]{2,0,1:T(8,128)}, u32[]{:S(2)}) copy-start(f32[32,3,256]{2,0,1:T(8,128)} %param.17) | copy-start | bytes 294916
  28.6 11.0 %copy-start.1 = (f32[32,3,256]{2,0,1:T(8,128)S(1)}, f32[32,3,256]{2,0,1:T(8,128)}, u32[]{:S(2)}) copy-start(f32[32,3,256]{2,0,1:T(8,128)} %param.19) | copy-start | bytes 294916
  28.6 11.0 %copy-start.2 = (s32[32,256]{1,0:T(8,128)S(1)}, s32[32,256]{1,0:T(8,128)}, u32[]{:S(2)}) copy-start(s32[32,256]{1,0:T(8,128)} %slot_ref.1) | copy-start | bytes 98308
  52.9 19.5 %copy-start.4 = (bf16[64,3,1024]{2,0,1:T(8,128)(2,1)S(1)}, bf16[64,3,1024]{2,0,1:T(8,128)(2,1)}, u32[]{:S(2)}) copy-start(bf16[64,3,1024]{2,0,1:T(8,128)(2,1)} %param.11) | copy-start | bytes 1179652
  53.0 8.9 %collective-permute-start.1 = (f32[24,128]{1,0:T(8,128)S(1)}, f32[24,128]{1,0:T(8,128)S(1)}, u32[]{:S(2)}, u32[]{:S(2)}) collective-permute-start(f32[24,128]{1,0:T(8,128)S(1)} %reduce_sum.57), channel_id=1, source_target_pairs={{0,488},{1,497},{2,506},{3,3},{4,12},{5,21},{6,30},{7,263},{8,496}... | collective-permute-start | bytes 36872 | tf_op jit(solution)/shard_map/ppermute | solution.py:341
